TPU v7x, 512 devices: a whole 4x4x16 slice. The times are simulated.
512 devices in a mesh: gx: 16 (over y, z_hi, core), gy: 32 (over x, z_lo).
Axes of the slice: x: 4, y: 4, z: 16 (z_hi: 2, z_lo: 8; z = z_hi * 8 + z_lo), core: 2. Of those that a mesh axis runs over, the one named last changes fastest.
Arguments:
- tokens: bfloat16 [512, 16384], P('gy', 'gx'), may hold values from -6 to 6
- gate_weight: bfloat16 [16384, 26624], P('gx', 'gy'), may hold values from -0.046875 to 0.046875
- up_weight: bfloat16 [16384, 26624], P('gx', 'gy'), may hold values from -0.046875 to 0.046875
- down_weight: bfloat16 [26624, 16384], P('gy', 'gx'), may hold values from -0.0390625 to 0.0390625
Outputs:
- mixed: bfloat16 [512, 16384], P('gy', 'gx')
All inputs are finite; a program needn't handle non-finite values.
Results may differ from a plain program's by a relative error of at most 0.0049.
Values may be sent and summed in bfloat16 or wider, within the bound.
No kernel may reach another device: no remote copies, remote signals or barrier semaphores. Data moves between devices by JAX's collectives and lax.ppermute only.
A program may use at most 64 MiB of HBM per device.

v0:
```python
import jax
import jax.numpy as jnp
from jax import lax
from jax.sharding import PartitionSpec as P


def on_device(tokens, gate_weight, up_weight, down_weight):
    piece = lax.all_gather(tokens, "gy", axis=0, tiled=True)
    gate_part = jnp.dot(piece, gate_weight, preferred_element_type=jnp.float32)
    up_part = jnp.dot(piece, up_weight, preferred_element_type=jnp.float32)
    partial_value = jnp.stack([gate_part, up_part])
    summed = lax.psum(partial_value, "gx")
    hidden = (jax.nn.silu(summed[0]) * summed[1]).astype(jnp.bfloat16)
    mixed = lax.psum_scatter(
        jnp.dot(hidden, down_weight, preferred_element_type=jnp.float32),
        "gy",
        scatter_dimension=0,
        tiled=True,
    )
    return mixed.astype(jnp.bfloat16)


def solution(mesh):
    return jax.shard_map(
        on_device,
        mesh=mesh,
        in_specs=(P("gy", "gx"), P("gx", "gy"), P("gx", "gy"), P("gy", "gx")),
        out_specs=P("gy", "gx"),
        check_vma=False,
    )
```

profile of v0, /device:TPU:16, one launch (start us, length us, event | category | flops | bytes accessed | tf_op | source)
XLA Modules:
  0.0 865.9 jit_solution(11074020991371853969)
XLA Ops:
  6.5 0.0 copy-start
  6.5 0.0 all-gather.2.cloned.1.call-start
  6.5 0.7 all-gather.2.cloned.1.call-update
  7.3 0.0 copy-start.1
  7.3 0.0 all-reduce.2.cloned.1.call-start
  7.3 228.6 %all-gather.2.cloned.1.call-done = bf16[512,1024]{1,0:T(8,128)(2,1)} async-done(((bf16[16,1024]{1,0:T(8,128)(2,1)}), bf16[512,1024]{1,0:T(8,128)(2,1)}) %all-gather.2.cloned.1.call-update) | async-done | bytes 1048592 | tf_op jit(solution)/shard_map/all_gather | solution.py:8
  235.9 0.0 copy-start.2
  235.9 2.9 convolution_bitcast_fusion
  238.9 0.0 copy-done.1
  238.9 0.0 copy-done.2
  238.9 1.1 convolution_bitcast_fusion.1
  240.0 2.1 pad_maximum_fusion
  242.1 0.0 all-reduce.2.cloned.1.call-update
  242.1 0.0 reduce-scatter.2.cloned.1.call-start
  242.2 363.3 %all-reduce.2.cloned.1.call-done = f32[2,512,832]{1,2,0:T(8,128)} async-done(((f32[2,512,832]{1,2,0:T(8,128)}), f32[2,512,832]{1,2,0:T(8,128)}) %all-reduce.2.cloned.1.call-update) | async-done | bytes 3407888 | tf_op jit(solution)/shard_map/psum | solution.py:12
  605.5 0.0 copy-done
  605.5 4.7 fusion.2
  610.2 0.0 reduce-scatter.2.cloned.1.call-update
  610.2 247.7 %reduce-scatter.2.cloned.1.call-done = f32[16,1024]{1,0:T(8,128)} async-done(((f32[512,1024]{1,0:T(8,128)}), f32[16,1024]{1,0:T(8,128)}) %reduce-scatter.2.cloned.1.call-update) | async-done | bytes 65552 | tf_op jit(solution)/shard_map/reduce_scatter | solution.py:14
  857.9 1.5 convert_element_type.7
Async XLA Ops:
  6.5 599.0 %copy-start = (bf16[832,1024]{1,0:T(8,128)(2,1)S(1)}, bf16[832,1024]{1,0:T(8,128)(2,1)}, u32[]{:S(2)}) copy-start(bf16[832,1024]{1,0:T(8,128)(2,1)} %param.7) | copy-start | bytes 5111812
  6.5 229.4 %all-gather.2.cloned.1.call-start = ((), (), s32[]{:S(2)}) async-start(), calls=%async_computation.1 | async-start | bytes 1081344 | tf_op jit(solution)/shard_map/all_gather | solution.py:8
  7.3 231.6 %copy-start.1 = (bf16[1024,832]{0,1:T(8,128)(2,1)S(1)}, bf16[1024,832]{0,1:T(8,128)(2,1)}, u32[]{:S(2)}) copy-start(bf16[1024,832]{0,1:T(8,128)(2,1)} %param.5) | copy-start | bytes 5111812
  7.3 598.2 %all-reduce.2.cloned.1.call-start = ((), (), s32[]{:S(2)}) async-start(), calls=%async_computation.2 | async-start | bytes 6815744 | tf_op jit(solution)/shard_map/psum | solution.py:12
  235.9 3.0 copy-start.2
  242.1 615.7 %reduce-scatter.2.cloned.1.call-start = ((), (), s32[]{:S(2)}) async-start(), calls=%async_computation.3 | async-start | bytes 2162688 | tf_op jit(solution)/shard_map/reduce_scatter | solution.py:14
Sparse Core Ops, SparseCore 0:
  9.4 226.4 all-gather.1
  242.3 363.1 all-reduce.1
  610.3 247.5 reduce-scatter.1
where the time goes:
time: 866 us
  waiting for transfers between devices  840 us (97%)
  between operations  13.1 us (2%)
  matrix products  8.7 us (1%)
    psum x1, waiting for transfers between devices, on_device(): summed = lax.psum(partial_value, 'gx')  363 us
    reduce_scatter x1, waiting for transfers between devices, on_device(): lax.psum_scatter(jnp.dot(hidden, down_weight, preferred_element_type=jnp....  248 us
    all_gather x1, waiting for transfers between devices, on_device(): piece = lax.all_gather(tokens, 'gy', axis=0, tiled=True)  229 us
  transfers between devices with their start and end apart: 3, of which 3 were waited for; matrix products, arithmetic and copies ran while one was open for 0% of the time, Pallas kernels for 0%

commit v1 on v0

v1 whole, which is shorter than its diff:
```python
import jax
import jax.numpy as jnp
from jax import lax
from jax.experimental import pallas as pl
from jax.experimental.pallas import tpu as pltpu
from jax.sharding import Mesh, PartitionSpec as P

GX = (("y", 4), ("zh", 2), ("c", 2))
GY = (("x", 4), ("zl", 8))
BF = jnp.bfloat16
F32 = jnp.float32
SWAP = [(0, 1), (1, 0)]
VMEM = pl.BlockSpec(memory_space=pltpu.VMEM)
SMEM = pl.BlockSpec(memory_space=pltpu.SMEM)


def gather(value, axis, size):
    return lax.all_to_all(jnp.broadcast_to(value[None], (size,) + value.shape), axis, 0, 0)


def add_up(parts):
    total = parts[0].astype(F32)
    for i in range(1, parts.shape[0]):
        total = total + parts[i].astype(F32)
    return total


def gate_up_kernel(half_ref, x_ref, g_ref, u_ref, out_ref):
    n = x_ref.shape[0] // 2
    start = pl.multiple_of(half_ref[0] * n, n)
    x = x_ref[pl.ds(start, n), :]
    for i, w in enumerate((g_ref, u_ref)):
        part = lax.dot_general(x, w[...], (((1,), (1,)), ((), ())), preferred_element_type=F32)
        out_ref[:, i] = part.reshape(out_ref.shape[0], out_ref.shape[2], out_ref.shape[3])


def gate_up(half, x, g, u):
    tokens, hidden = x.shape[0], g.shape[0]
    return pl.pallas_call(
        gate_up_kernel,
        out_shape=jax.ShapeDtypeStruct((4, 2, tokens // 8, hidden), F32),
        in_specs=[SMEM, VMEM, VMEM, VMEM],
        out_specs=VMEM,
        cost_estimate=pl.CostEstimate(flops=2 * tokens * x.shape[1] * hidden, bytes_accessed=8 << 20, transcendentals=0),
        compiler_params=pltpu.CompilerParams(vmem_limit_bytes=16 << 20),
        name="gate_up",
    )(half, x, g, u)


def down_kernel(half_ref, mine_ref, far_ref, w_ref, out_ref):
    n = mine_ref.shape[0]
    for h, start in ((mine_ref, half_ref[0] * n), (far_ref, (1 - half_ref[0]) * n)):
        part = jnp.dot(h[...], w_ref[...], preferred_element_type=F32)
        out_ref[pl.ds(pl.multiple_of(start, n), n), :] = part.astype(BF)


def down(half, mine, far, w):
    n, hidden = mine.shape
    return pl.pallas_call(
        down_kernel,
        out_shape=jax.ShapeDtypeStruct((2 * n, w.shape[1]), BF),
        in_specs=[SMEM, VMEM, VMEM, VMEM],
        out_specs=VMEM,
        cost_estimate=pl.CostEstimate(flops=4 * n * hidden * w.shape[1], bytes_accessed=4 << 20, transcendentals=0),
        compiler_params=pltpu.CompilerParams(vmem_limit_bytes=16 << 20),
        name="down",
    )(half, mine, far, w)


def on_device(tokens, gate_weight, up_weight, down_weight):
    rows, width = tokens.shape
    hidden_units = gate_weight.shape[1]
    half = lax.axis_index("c").astype(jnp.int32).reshape(1)
    piece = gather(tokens, "zl", 8).reshape(8 * rows, width)
    piece = gather(piece, "x", 4).reshape(32 * rows, width)

    other = gate_up(1 - half, piece, gate_weight.T, up_weight.T)
    other = lax.ppermute(other, "c", SWAP)
    mine = gate_up(half, piece, gate_weight.T, up_weight.T)
    parts = lax.all_to_all((mine + other).astype(BF), "y", 0, 0)
    summed = add_up(parts)
    summed = summed + lax.ppermute(summed.astype(BF), "zh", SWAP).astype(F32)

    hidden = (jax.nn.silu(summed[0]) * summed[1]).astype(BF)
    hidden = gather(hidden, "y", 4).reshape(16 * rows, hidden_units)
    far = lax.ppermute(hidden, "c", SWAP)

    out = down(half, hidden, far, down_weight)
    out = add_up(lax.all_to_all(out.reshape(4, 8 * rows, width), "x", 0, 0))
    out = add_up(lax.all_to_all(out.reshape(8, rows, width), "zl", 0, 0))
    return out.astype(BF)


def solution(mesh):
    sizes = [n for _, n in GX + GY]
    names = [a for a, _ in GX + GY]
    fine = Mesh(mesh.devices.reshape(sizes), names)
    gx, gy = tuple(a for a, _ in GX), tuple(a for a, _ in GY)
    return jax.shard_map(
        on_device,
        mesh=fine,
        in_specs=(P(gy, gx), P(gx, gy), P(gx, gy), P(gy, gx)),
        out_specs=P(gy, gx),
        check_vma=False,
    )
```

time: 866 us -> 177 us (0.20)
  the two profiles are of different devices: /device:TPU:16 before, /device:TPU:2 now
where the time goes in v1:
time: 177 us; the launch traced here: 176 us
  blocking collectives  126 us (71%)
  waiting for transfers between devices  24.4 us (14%)
  starting transfers between devices  17 us (10%)
  Pallas kernels  3.8 us (2%)
  local copies, waits for them, and re-layouts  3.37 us (2%)
    all_to_all x1, blocking collectives, on_device(): out = add_up(lax.all_to_all(out.reshape(8, rows, width), 'zl', 0, 0))  50.8 us
    all_to_all x2, blocking collectives, gather(): lax.all_to_all(jnp.broadcast_to(value[None], (size,) + value.shape), axis...  39.1 us
    all_to_all x1, blocking collectives, on_device(): parts = lax.all_to_all((mine + other).astype(BF), 'y', 0, 0)  18.3 us
    all_to_all x1, blocking collectives, on_device(): out = add_up(lax.all_to_all(out.reshape(4, 8 * rows, width), 'x', 0, 0))  18.1 us
    ppermute x1, waiting for transfers between devices, on_device(): summed = summed + lax.ppermute(summed.astype(BF), 'zh', SWAP).astype(F32)  10.8 us
    all_to_all x1, waiting for transfers between devices, gather(): lax.all_to_all(jnp.broadcast_to(value[None], (size,) + value.shape), axis...  9.43 us
    ppermute x1, starting transfers between devices, on_device(): summed = summed + lax.ppermute(summed.astype(BF), 'zh', SWAP).astype(F32)  8.35 us
    all_to_all x1, starting transfers between devices, gather(): lax.all_to_all(jnp.broadcast_to(value[None], (size,) + value.shape), axis...  4.82 us
  transfers between devices with their start and end apart: 4, of which 4 were waited for; matrix products, arithmetic and copies ran while one was open for 0% of the time, Pallas kernels for 1%

profile of v1, /device:TPU:2, one launch (start us, length us, event | category | flops | bytes accessed | tf_op | source)
XLA Modules:
  0.0 176.3 jit_solution(4065856980736545816)
XLA Ops:
  0.0 0.8 broadcast_in_dim.10
  0.8 29.0 %all_to_all.30 = bf16[8,16,1024]{2,1,0:T(8,128)(2,1)S(1)} all-to-all(bf16[8,16,1024]{2,1,0:T(8,128)(2,1)S(1)} %broadcast_in_dim.10), channel_id=1, replica_groups=mesh['y'=4,'zh'=2,'c'=2,'x'=4,'zl'=8] {'zl'}, dimensions={0} | all-to-all | bytes 524288 | tf_op jit(solution)/shard_map/all_to_all | solution.py:18
  29.8 0.0 copy-start
  29.8 1.1 broadcast_in_dim.23
  30.9 4.8 %all-to-all-start.1 = ((bf16[4,128,1024]{2,1,0:T(8,128)(2,1)}), bf16[4,128,1024]{2,1,0:T(8,128)(2,1)S(1)}, u32[]{:S(2)}, u32[]{:S(2)}) async-start(bf16[4,128,1024]{2,1,0:T(8,128)(2,1)} %broadcast_in_dim.23), calls=%async_computation.1 | async-start | bytes 2097152 | tf_op jit(solution)/shard_map/all_to_all | solution.py:18
  35.7 9.4 %all-to-all-done.1 = bf16[4,128,1024]{2,1,0:T(8,128)(2,1)S(1)} async-done(((bf16[4,128,1024]{2,1,0:T(8,128)(2,1)}), bf16[4,128,1024]{2,1,0:T(8,128)(2,1)S(1)}, u32[]{:S(2)}, u32[]{:S(2)}) %all-to-all-start.1) | async-done | bytes 1048608 | tf_op jit(solution)/shard_map/all_to_all | solution.py:18
  45.1 0.0 copy-done
  45.1 0.0 copy-start.1
  45.2 1.5 copy-done.1
  46.6 0.0 copy-start.2
  46.6 1.3 gate_up.3
  47.9 1.9 %collective-permute-start = (f32[4,2,64,832]{3,2,1,0:T(8,128)S(1)}, f32[4,2,64,832]{3,2,1,0:T(8,128)S(1)}, u32[]{:S(2)}, u32[]{:S(2)}) collective-permute-start(f32[4,2,64,832]{3,2,1,0:T(8,128)S(1)} %gate_up.3), channel_id=1, source_target_pairs={{0,32},{32,0},{1,33},{33,1},{2,34},{34,2},{3,35},{35,3},{4,36},{36... | collective-permute-start | bytes 5111816 | tf_op jit(solution)/shard_map/ppermute | solution.py:78
  49.8 0.0 copy-done.2
  49.8 1.3 gate_up.2
  51.1 2.5 %collective-permute-done = f32[4,2,64,832]{3,2,1,0:T(8,128)S(1)} collective-permute-done((f32[4,2,64,832]{3,2,1,0:T(8,128)S(1)}, f32[4,2,64,832]{3,2,1,0:T(8,128)S(1)}, u32[]{:S(2)}, u32[]{:S(2)}) %collective-permute-start) | collective-permute-done | bytes 1703968 | tf_op jit(solution)/shard_map/ppermute | solution.py:78
  53.6 0.2 add_convert_fusion
  53.8 18.3 %all_to_all.31 = bf16[4,2,64,832]{3,2,1,0:T(8,128)(2,1)S(1)} all-to-all(bf16[4,2,64,832]{3,2,1,0:T(8,128)(2,1)S(1)} %add_convert_fusion), channel_id=1, replica_groups=mesh['y'=4,'zh'=2,'c'=2,'x'=4,'zl'=8] {'y'}, dimensions={0} | all-to-all | bytes 1703936 | tf_op jit(solution)/shard_map/all_to_all | solution.py:80
  72.1 0.1 bitcast_convert_fusion
  72.2 0.0 copy-start.3
  72.2 8.4 %collective-permute-start.1 = (bf16[2,64,832]{2,1,0:T(8,128)(2,1)S(1)}, bf16[2,64,832]{2,1,0:T(8,128)(2,1)S(1)}, u32[]{:S(2)}, u32[]{:S(2)}) collective-permute-start(bf16[2,64,832]{2,1,0:T(8,128)(2,1)S(1)} %bitcast_convert_fusion), channel_id=1, source_target_pairs={{0,64},{64,0},{1,65},{65,1},{2,66},{66,2},{3,67},{67,3},{4,68},{68... | collective-permute-start | bytes 638984 | tf_op jit(solution)/shard_map/ppermute | solution.py:82
  80.6 10.8 %collective-permute-done.1 = bf16[2,64,832]{2,1,0:T(8,128)(2,1)S(1)} collective-permute-done((bf16[2,64,832]{2,1,0:T(8,128)(2,1)S(1)}, bf16[2,64,832]{2,1,0:T(8,128)(2,1)S(1)}, u32[]{:S(2)}, u32[]{:S(2)}) %collective-permute-start.1) | collective-permute-done | bytes 213024 | tf_op jit(solution)/shard_map/ppermute | solution.py:82
  91.3 0.1 bitcast_add_fusion
  91.5 0.1 fusion.1
  91.6 10.1 %all_to_all.32 = bf16[4,64,832]{2,1,0:T(8,128)(2,1)S(1)} all-to-all(bf16[4,64,832]{2,1,0:T(8,128)(2,1)S(1)} %broadcast_in_dim.25), channel_id=1, replica_groups=mesh['y'=4,'zh'=2,'c'=2,'x'=4,'zl'=8] {'y'}, dimensions={0} | all-to-all | bytes 851968 | tf_op jit(solution)/shard_map/all_to_all | solution.py:18
  101.7 1.9 %collective-permute-start.2 = (bf16[256,832]{1,0:T(8,128)(2,1)S(1)}, bf16[256,832]{1,0:T(8,128)(2,1)S(1)}, u32[]{:S(2)}, u32[]{:S(2)}) collective-permute-start(bf16[256,832]{1,0:T(8,128)(2,1)S(1)} %bitcast.22), channel_id=1, source_target_pairs={{0,32},{32,0},{1,33},{33,1},{2,34},{34,2},{3,35},{35,3},{4,36},{36... | collective-permute-start | bytes 1277960 | tf_op jit(solution)/shard_map/ppermute | solution.py:86
  103.6 1.8 %collective-permute-done.2.far_ref = bf16[256,832]{1,0:T(8,128)(2,1)S(1)} collective-permute-done((bf16[256,832]{1,0:T(8,128)(2,1)S(1)}, bf16[256,832]{1,0:T(8,128)(2,1)S(1)}, u32[]{:S(2)}, u32[]{:S(2)}) %collective-permute-start.2) | collective-permute-done | bytes 426016 | tf_op jit(solution)/shard_map/ppermute | solution.py:86
  105.4 0.0 copy-done.3
  105.4 1.2 down.1
  106.7 18.1 %all_to_all.33 = bf16[4,128,1024]{2,1,0:T(8,128)(2,1)S(1)} all-to-all(bf16[4,128,1024]{2,1,0:T(8,128)(2,1)S(1)} %bitcast.21), channel_id=1, replica_groups=mesh['y'=4,'zh'=2,'c'=2,'x'=4,'zl'=8] {'x'}, dimensions={0} | all-to-all | bytes 2097152 | tf_op jit(solution)/shard_map/all_to_all | solution.py:89
  124.8 0.2 convert_add_fusion
  125.0 50.8 %all_to_all.34 = f32[8,16,1024]{2,1,0:T(8,128)S(1)} all-to-all(f32[8,16,1024]{2,1,0:T(8,128)S(1)} %bitcast.24), channel_id=1, replica_groups=mesh['y'=4,'zh'=2,'c'=2,'x'=4,'zl'=8] {'zl'}, dimensions={0} | all-to-all | bytes 1048576 | tf_op jit(solution)/shard_map/all_to_all | solution.py:90
  175.7 0.6 fusion.3
  (1 shorter events, 0.0 us)
Async XLA Ops:
  29.8 15.4 %copy-start = (bf16[1024,832]{0,1:T(8,128)(2,1)S(1)}, bf16[1024,832]{0,1:T(8,128)(2,1)}, u32[]{:S(2)}) copy-start(bf16[1024,832]{0,1:T(8,128)(2,1)} %param.5) | copy-start | bytes 5111812
  30.9 14.3 %all-to-all-start.1 = ((bf16[4,128,1024]{2,1,0:T(8,128)(2,1)}), bf16[4,128,1024]{2,1,0:T(8,128)(2,1)S(1)}, u32[]{:S(2)}, u32[]{:S(2)}) async-start(bf16[4,128,1024]{2,1,0:T(8,128)(2,1)} %broadcast_in_dim.23), calls=%async_computation.1 | async-start | bytes 2097152 | tf_op jit(solution)/shard_map/all_to_all | solution.py:18
  45.1 1.5 copy-start.1
  46.6 3.2 %copy-start.2 = (bf16[1024,832]{0,1:T(8,128)(2,1)S(1)}, bf16[1024,832]{0,1:T(8,128)(2,1)}, u32[]{:S(2)}) copy-start(bf16[1024,832]{0,1:T(8,128)(2,1)} %param.6) | copy-start | bytes 5111812
  47.9 5.7 %collective-permute-start = (f32[4,2,64,832]{3,2,1,0:T(8,128)S(1)}, f32[4,2,64,832]{3,2,1,0:T(8,128)S(1)}, u32[]{:S(2)}, u32[]{:S(2)}) collective-permute-start(f32[4,2,64,832]{3,2,1,0:T(8,128)S(1)} %gate_up.3), channel_id=1, source_target_pairs={{0,32},{32,0},{1,33},{33,1},{2,34},{34,2},{3,35},{35,3},{4,36},{36... | collective-permute-start | bytes 5111816 | tf_op jit(solution)/shard_map/ppermute | solution.py:78
  72.2 33.2 %copy-start.3 = (bf16[832,1024]{1,0:T(8,128)(2,1)S(1)}, bf16[832,1024]{1,0:T(8,128)(2,1)}, u32[]{:S(2)}) copy-start(bf16[832,1024]{1,0:T(8,128)(2,1)} %w_ref.1) | copy-start | bytes 5111812
  72.2 19.1 %collective-permute-start.1 = (bf16[2,64,832]{2,1,0:T(8,128)(2,1)S(1)}, bf16[2,64,832]{2,1,0:T(8,128)(2,1)S(1)}, u32[]{:S(2)}, u32[]{:S(2)}) collective-permute-start(bf16[2,64,832]{2,1,0:T(8,128)(2,1)S(1)} %bitcast_convert_fusion), channel_id=1, source_target_pairs={{0,64},{64,0},{1,65},{65,1},{2,66},{66,2},{3,67},{67,3},{4,68},{68... | collective-permute-start | bytes 638984 | tf_op jit(solution)/shard_map/ppermute | solution.py:82
  101.7 3.7 %collective-permute-start.2 = (bf16[256,832]{1,0:T(8,128)(2,1)S(1)}, bf16[256,832]{1,0:T(8,128)(2,1)S(1)}, u32[]{:S(2)}, u32[]{:S(2)}) collective-permute-start(bf16[256,832]{1,0:T(8,128)(2,1)S(1)} %bitcast.22), channel_id=1, source_target_pairs={{0,32},{32,0},{1,33},{33,1},{2,34},{34,2},{3,35},{35,3},{4,36},{36... | collective-permute-start | bytes 1277960 | tf_op jit(solution)/shard_map/ppermute | solution.py:86

commit v2 on v1

v2 whole, which is shorter than its diff:
```python
import jax
import jax.numpy as jnp
from jax import lax
from jax.experimental import pallas as pl
from jax.experimental.pallas import tpu as pltpu
from jax.sharding import Mesh, PartitionSpec as P

GX = (("y", 4), ("zh", 2), ("c", 2))
BF = jnp.bfloat16
F32 = jnp.float32
SWAP = [(0, 1), (1, 0)]
VMEM = pl.BlockSpec(memory_space=pltpu.VMEM)
SMEM = pl.BlockSpec(memory_space=pltpu.SMEM)
ZSPLIT = True
ZB, NB = ("zq", 4) if ZSPLIT else ("zl", 8)
XA = ("x", "zp") if ZSPLIT else "x"
GY = (("x", 4), ("zq", 4), ("zp", 2)) if ZSPLIT else (("x", 4), ("zl", 8))


def gather(value, axis, size):
    return lax.all_to_all(jnp.broadcast_to(value[None], (size,) + value.shape), axis, 0, 0)


def scatter_sum(terms, axis, me, own):
    terms, own = lax.optimization_barrier((terms, own))
    parts = lax.all_to_all(terms, axis, 0, 0)
    for part, far in zip(parts, me):
        own = own + jnp.where(far, part.astype(F32), 0.0)
    return own


def at(terms, me):
    return lax.dynamic_index_in_dim(terms, me, 0, keepdims=False, allow_negative_indices=False)


def gate_up_kernel(core_ref, x_ref, g_ref, u_ref, out_ref):
    y, _, rows, width = x_ref.shape
    x = x_ref[:, core_ref[0]].reshape(y * rows, width)
    for i, w in enumerate((g_ref, u_ref)):
        part = lax.dot_general(x, w[...], (((1,), (1,)), ((), ())), preferred_element_type=F32)
        n = part.shape[1]
        out_ref[:, :, i * n : (i + 1) * n] = part.reshape(y, rows, n)


def gate_up(core, x, g, u):
    y, _, rows, width = x.shape
    hidden = g.shape[0]
    return pl.pallas_call(
        gate_up_kernel,
        out_shape=jax.ShapeDtypeStruct((y, rows, 2 * hidden), F32),
        in_specs=[SMEM, VMEM, VMEM, VMEM],
        out_specs=VMEM,
        cost_estimate=pl.CostEstimate(flops=4 * y * rows * width * hidden, bytes_accessed=8 << 20, transcendentals=0),
        compiler_params=pltpu.CompilerParams(vmem_limit_bytes=16 << 20),
        name="gate_up",
    )(core, x, g, u)


def down_kernel(x_at_ref, h_ref, w_ref, out_ref, own_ref, sums):
    sums[...] = jnp.dot(h_ref[...], w_ref[...], preferred_element_type=F32)
    out_ref[...] = sums[...].astype(BF)
    n = own_ref.shape[0]
    own_ref[...] = sums[pl.ds(pl.multiple_of(x_at_ref[0] * n, n), n), :]


def down(x_at, h, w):
    n, hidden = h.shape
    return pl.pallas_call(
        down_kernel,
        out_shape=[jax.ShapeDtypeStruct((n, w.shape[1]), BF), jax.ShapeDtypeStruct((n // (32 // NB), w.shape[1]), F32)],
        in_specs=[SMEM, VMEM, VMEM],
        out_specs=[VMEM, VMEM],
        scratch_shapes=[pltpu.VMEM((n, w.shape[1]), F32)],
        cost_estimate=pl.CostEstimate(flops=2 * n * hidden * w.shape[1], bytes_accessed=4 << 20, transcendentals=0),
        compiler_params=pltpu.CompilerParams(vmem_limit_bytes=16 << 20),
        name="down",
    )(x_at, h, w)


def on_device(tokens, gate_weight, up_weight, down_weight):
    rows, width = tokens.shape
    hidden_units = gate_weight.shape[1]
    place = {a: lax.axis_index(a).astype(jnp.int32) for a in ("y", "c", "x", ZB)}
    place["xa"] = place["x"] * 2 + lax.axis_index("zp") if ZSPLIT else place["x"]
    far_from = {a: [place[a] != i for i in range(n)] for a, n in (("y", 4), ("xa", 32 // NB), (ZB, NB))}
    core, first = place["c"].reshape(1), place["c"] == 0
    place, far_from, core, other_core, first, tokens = lax.optimization_barrier(
        (place, far_from, core, 1 - core, first, tokens)
    )
    piece = gather(tokens, ZB, NB).reshape(NB * rows, width)
    piece = gather(piece, XA, 32 // NB).reshape(4, 2, 4 * rows, width)

    other = gate_up(other_core, piece, gate_weight.T, up_weight.T)
    other = lax.ppermute(other, "c", SWAP)
    mine = gate_up(core, piece, gate_weight.T, up_weight.T)
    y = place["y"]
    summed = scatter_sum((mine + other).astype(BF), "y", far_from["y"], at(mine, y) + at(other, y))
    summed = summed + lax.ppermute(summed.astype(BF), "zh", SWAP).astype(F32)

    hidden = (jax.nn.silu(summed[:, :hidden_units]) * summed[:, hidden_units:]).astype(BF)
    hidden = gather(hidden, "y", 4)
    far = lax.ppermute(hidden, "c", SWAP)
    hidden = jnp.stack([jnp.where(first, hidden, far), jnp.where(first, far, hidden)], axis=1)
    hidden = hidden.reshape(32 * rows, hidden_units)

    out, own = down(place["xa"].reshape(1), hidden, down_weight)
    out = scatter_sum(out.reshape(32 // NB, NB * rows, width), XA, far_from["xa"], own)
    out = out.reshape(NB, rows, width)
    out = scatter_sum(out.astype(BF), ZB, far_from[ZB], at(out, place[ZB]))
    return out.astype(BF)


def solution(mesh):
    sizes = [n for _, n in GX + GY]
    names = [a for a, _ in GX + GY]
    fine = Mesh(mesh.devices.reshape(sizes), names)
    gx, gy = tuple(a for a, _ in GX), tuple(a for a, _ in GY)
    return jax.shard_map(
        on_device,
        mesh=fine,
        in_specs=(P(gy, gx), P(gx, gy), P(gx, gy), P(gy, gx)),
        out_specs=P(gy, gx),
        check_vma=False,
    )
```

time: 177 us -> 150 us (0.85)
  blocking collectives: 126 us -> 111 us
  starting transfers between devices: 17 us -> 12.2 us
  waiting for transfers between devices: 24.4 us -> 19.6 us
  local copies, waits for them, and re-layouts: 3.37 us -> 0.94 us
    all_to_all x3, blocking collectives: 87.1 us -> 61.3 us  [scatter_sum(): parts = lax.all_to_all(terms, axis, 0, 0)]
    all_to_all x2 -> x3, blocking collectives: 39.1 us -> 49.8 us  [gather(): lax.all_to_all(jnp.broadcast_to(value[None], (size,) + value.shape), axis...]
    all_to_all x1 -> x0, waiting for transfers between devices: 9.43 us -> none  [gather(): lax.all_to_all(jnp.broadcast_to(value[None], (size,) + value.shape), axis...]
    ppermute x1, waiting for transfers between devices: 10.8 us -> 15.7 us  [on_device(): summed = summed + lax.ppermute(summed.astype(BF), 'zh', SWAP).astype(F32)]
    all_to_all x1 -> x0, starting transfers between devices: 4.82 us -> none  [gather(): lax.all_to_all(jnp.broadcast_to(value[None], (size,) + value.shape), axis...]
  transfers between devices with their start and end apart: 4 -> 3, of which waited for: 4 -> 3; matrix products, arithmetic and copies ran while one was open for 0% -> 0% of each run, Pallas kernels for 1% -> 1%
where the time goes in v2:
time: 150 us
  blocking collectives  111 us (74%)
  waiting for transfers between devices  19.6 us (13%)
  starting transfers between devices  12.2 us (8%)
  Pallas kernels  4.05 us (3%)
  other arithmetic  1.67 us (1%)
    all_to_all x3, blocking collectives, scatter_sum(): parts = lax.all_to_all(terms, axis, 0, 0)  61.3 us
    all_to_all x3, blocking collectives, gather(): lax.all_to_all(jnp.broadcast_to(value[None], (size,) + value.shape), axis...  49.8 us
    ppermute x1, waiting for transfers between devices, on_device(): summed = summed + lax.ppermute(summed.astype(BF), 'zh', SWAP).astype(F32)  15.7 us
    ppermute x1, starting transfers between devices, on_device(): summed = summed + lax.ppermute(summed.astype(BF), 'zh', SWAP).astype(F32)  8.25 us
  transfers between devices with their start and end apart: 3, of which 3 were waited for; matrix products, arithmetic and copies ran while one was open for 0% of the time, Pallas kernels for 1%

profile of v2, /device:TPU:2, one launch (start us, length us, event | category | flops | bytes accessed | tf_op | source)
XLA Modules:
  0.0 149.7 jit_solution(2647185023792482292)
XLA Ops:
  0.0 0.8 broadcast_in_dim.44
  0.8 0.0 copy-start.1
  0.8 23.3 %all_to_all.30 = bf16[4,16,1024]{2,1,0:T(8,128)(2,1)S(1)} all-to-all(bf16[4,16,1024]{2,1,0:T(8,128)(2,1)S(1)} %broadcast_in_dim.44), channel_id=1, replica_groups=mesh['y'=4,'zh'=2,'c'=2,'x'=4,'zq'=4,'zp'=2] {'zq'}, dimensions={0} | all-to-all | bytes 262144 | tf_op jit(solution)/shard_map/all_to_all | solution.py:21
  24.1 0.0 copy-start
  24.1 0.1 broadcast_in_dim.46
  24.2 16.4 %all_to_all.31 = bf16[8,64,1024]{2,1,0:T(8,128)(2,1)S(1)} all-to-all(bf16[8,64,1024]{2,1,0:T(8,128)(2,1)S(1)} %broadcast_in_dim.46), channel_id=1, replica_groups=mesh['y'=4,'zh'=2,'c'=2,'x'=4,'zq'=4,'zp'=2] {'x','zp'}, dimensions={0} | all-to-all | bytes 2097152 | tf_op jit(solution)/shard_map/all_to_all | solution.py:21
  40.6 0.0 copy-done.1
  40.6 0.0 copy-done
  40.6 1.4 gate_up.3
  42.0 1.9 %collective-permute-start = (f32[4,64,1664]{2,1,0:T(8,128)S(1)}, f32[4,64,1664]{2,1,0:T(8,128)S(1)}, u32[]{:S(2)}, u32[]{:S(2)}) collective-permute-start(f32[4,64,1664]{2,1,0:T(8,128)S(1)} %gate_up.3), channel_id=1, source_target_pairs={{0,32},{32,0},{1,33},{33,1},{2,34},{34,2},{3,35},{35,3},{4,36},{36... | collective-permute-start | bytes 5111816 | tf_op jit(solution)/shard_map/ppermute | solution.py:94
  43.9 1.4 gate_up.2
  45.3 2.2 %collective-permute-done = f32[4,64,1664]{2,1,0:T(8,128)S(1)} collective-permute-done((f32[4,64,1664]{2,1,0:T(8,128)S(1)}, f32[4,64,1664]{2,1,0:T(8,128)S(1)}, u32[]{:S(2)}, u32[]{:S(2)}) %collective-permute-start) | collective-permute-done | bytes 1703968 | tf_op jit(solution)/shard_map/ppermute | solution.py:94
  47.5 0.2 add_convert_fusion
  47.7 0.1 add_bitcast_fusion
  47.7 17.6 %all_to_all.32 = bf16[4,64,1664]{2,1,0:T(8,128)(2,1)S(1)} all-to-all(bf16[4,64,1664]{2,1,0:T(8,128)(2,1)S(1)} %add_convert_fusion), channel_id=1, replica_groups=mesh['y'=4,'zh'=2,'c'=2,'x'=4,'zq'=4,'zp'=2] {'y'}, dimensions={0} | all-to-all | bytes 1703936 | tf_op jit(solution)/shard_map/all_to_all | solution.py:26
  65.3 0.2 fusion.2
  65.5 8.3 %collective-permute-start.1 = (bf16[64,1664]{1,0:T(8,128)(2,1)S(1)}, bf16[64,1664]{1,0:T(8,128)(2,1)S(1)}, u32[]{:S(2)}, u32[]{:S(2)}) collective-permute-start(bf16[64,1664]{1,0:T(8,128)(2,1)S(1)} %get-tuple-element.67), channel_id=1, source_target_pairs={{0,64},{64,0},{1,65},{65,1},{2,66},{66,2},{3,67},{67,3},{4,68},{68... | collective-permute-start | bytes 638984 | tf_op jit(solution)/shard_map/ppermute | solution.py:98
  73.7 15.7 %collective-permute-done.1 = bf16[64,1664]{1,0:T(8,128)(2,1)S(1)} collective-permute-done((bf16[64,1664]{1,0:T(8,128)(2,1)S(1)}, bf16[64,1664]{1,0:T(8,128)(2,1)S(1)}, u32[]{:S(2)}, u32[]{:S(2)}) %collective-permute-start.1) | collective-permute-done | bytes 213024 | tf_op jit(solution)/shard_map/ppermute | solution.py:98
  89.4 0.1 fusion
  89.6 10.1 %all_to_all.33 = bf16[4,64,832]{2,1,0:T(8,128)(2,1)S(1)} all-to-all(bf16[4,64,832]{2,1,0:T(8,128)(2,1)S(1)} %broadcast_in_dim.48), channel_id=1, replica_groups=mesh['y'=4,'zh'=2,'c'=2,'x'=4,'zq'=4,'zp'=2] {'y'}, dimensions={0} | all-to-all | bytes 851968 | tf_op jit(solution)/shard_map/all_to_all | solution.py:21
  99.7 0.0 copy-start.2
  99.7 2.0 %collective-permute-start.2 = (bf16[4,64,832]{2,1,0:T(8,128)(2,1)S(1)}, bf16[4,64,832]{2,1,0:T(8,128)(2,1)S(1)}, u32[]{:S(2)}, u32[]{:S(2)}) collective-permute-start(bf16[4,64,832]{2,1,0:T(8,128)(2,1)S(1)} %all_to_all.33), channel_id=1, source_target_pairs={{0,32},{32,0},{1,33},{33,1},{2,34},{34,2},{3,35},{35,3},{4,36},{36... | collective-permute-start | bytes 1277960 | tf_op jit(solution)/shard_map/ppermute | solution.py:102
  101.8 1.8 %collective-permute-done.2 = bf16[4,64,832]{2,1,0:T(8,128)(2,1)S(1)} collective-permute-done((bf16[4,64,832]{2,1,0:T(8,128)(2,1)S(1)}, bf16[4,64,832]{2,1,0:T(8,128)(2,1)S(1)}, u32[]{:S(2)}, u32[]{:S(2)}) %collective-permute-start.2) | collective-permute-done | bytes 426016 | tf_op jit(solution)/shard_map/ppermute | solution.py:102
  103.5 0.1 select_bitcast_fusion.1
  103.6 0.1 pad_maximum_fusion
  103.8 0.0 copy-done.2
  103.8 1.3 down.1
  105.1 22.4 %all_to_all.34 = bf16[8,64,1024]{2,1,0:T(8,128)(2,1)S(1)} all-to-all(bf16[8,64,1024]{2,1,0:T(8,128)(2,1)S(1)} %bitcast.89), channel_id=1, replica_groups=mesh['y'=4,'zh'=2,'c'=2,'x'=4,'zq'=4,'zp'=2] {'x','zp'}, dimensions={0} | all-to-all | bytes 2097152 | tf_op jit(solution)/shard_map/all_to_all | solution.py:26
  127.5 0.2 bitcast_add_fusion.4
  127.7 21.4 %all_to_all.35 = bf16[4,16,1024]{2,1,0:T(8,128)(2,1)S(1)} all-to-all(bf16[4,16,1024]{2,1,0:T(8,128)(2,1)S(1)} %convert_element_type.98), channel_id=1, replica_groups=mesh['y'=4,'zh'=2,'c'=2,'x'=4,'zq'=4,'zp'=2] {'zq'}, dimensions={0} | all-to-all | bytes 262144 | tf_op jit(solution)/shard_map/all_to_all | solution.py:26
  149.1 0.6 fusion.1
  (4 shorter events, 0.1 us)
Async XLA Ops:
  0.8 39.8 %copy-start.1 = (bf16[1024,832]{0,1:T(8,128)(2,1)S(1)}, bf16[1024,832]{0,1:T(8,128)(2,1)}, u32[]{:S(2)}) copy-start(bf16[1024,832]{0,1:T(8,128)(2,1)} %param.6) | copy-start | bytes 5111812
  24.1 16.5 %copy-start = (bf16[1024,832]{0,1:T(8,128)(2,1)S(1)}, bf16[1024,832]{0,1:T(8,128)(2,1)}, u32[]{:S(2)}) copy-start(bf16[1024,832]{0,1:T(8,128)(2,1)} %param.5) | copy-start | bytes 5111812
  42.0 5.5 %collective-permute-start = (f32[4,64,1664]{2,1,0:T(8,128)S(1)}, f32[4,64,1664]{2,1,0:T(8,128)S(1)}, u32[]{:S(2)}, u32[]{:S(2)}) collective-permute-start(f32[4,64,1664]{2,1,0:T(8,128)S(1)} %gate_up.3), channel_id=1, source_target_pairs={{0,32},{32,0},{1,33},{33,1},{2,34},{34,2},{3,35},{35,3},{4,36},{36... | collective-permute-start | bytes 5111816 | tf_op jit(solution)/shard_map/ppermute | solution.py:94
  65.5 23.9 %collective-permute-start.1 = (bf16[64,1664]{1,0:T(8,128)(2,1)S(1)}, bf16[64,1664]{1,0:T(8,128)(2,1)S(1)}, u32[]{:S(2)}, u32[]{:S(2)}) collective-permute-start(bf16[64,1664]{1,0:T(8,128)(2,1)S(1)} %get-tuple-element.67), channel_id=1, source_target_pairs={{0,64},{64,0},{1,65},{65,1},{2,66},{66,2},{3,67},{67,3},{4,68},{68... | collective-permute-start | bytes 638984 | tf_op jit(solution)/shard_map/ppermute | solution.py:98
  99.7 4.1 %copy-start.2 = (bf16[832,1024]{1,0:T(8,128)(2,1)S(1)}, bf16[832,1024]{1,0:T(8,128)(2,1)}, u32[]{:S(2)}) copy-start(bf16[832,1024]{1,0:T(8,128)(2,1)} %w_ref.1) | copy-start | bytes 5111812
  99.7 3.8 %collective-permute-start.2 = (bf16[4,64,832]{2,1,0:T(8,128)(2,1)S(1)}, bf16[4,64,832]{2,1,0:T(8,128)(2,1)S(1)}, u32[]{:S(2)}, u32[]{:S(2)}) collective-permute-start(bf16[4,64,832]{2,1,0:T(8,128)(2,1)S(1)} %all_to_all.33), channel_id=1, source_target_pairs={{0,32},{32,0},{1,33},{33,1},{2,34},{34,2},{3,35},{35,3},{4,36},{36... | collective-permute-start | bytes 1277960 | tf_op jit(solution)/shard_map/ppermute | solution.py:102

commit v3 on v0

v3 whole, which is shorter than its diff:
```python
import jax
import jax.numpy as jnp
from jax import lax
from jax.experimental import pallas as pl
from jax.experimental.pallas import tpu as pltpu
from jax.sharding import Mesh, PartitionSpec as P


GX = (("y", 4), ("zh", 2), ("c", 2))
GY = (("x", 4), ("zq", 4), ("zp", 2))
NEAR = ("x", "zp")
FAR = ("zq", "c")
BF = jnp.bfloat16
F32 = jnp.float32
LAST = BF
SWAP = [(0, 1), (1, 0)]
VMEM = pl.BlockSpec(memory_space=pltpu.VMEM)
SMEM = pl.BlockSpec(memory_space=pltpu.SMEM)
HBM = pl.BlockSpec(memory_space=pltpu.HBM)


def params(mib):
    return pltpu.CompilerParams(vmem_limit_bytes=mib << 20)


def add_far(parts, far, own):
    for i, is_far in enumerate(far):
        own = own + jnp.where(is_far, parts[i].astype(F32), 0.0)
    return own


def gate_up_kernel(place_ref, x_ref, *refs):
    weights, (out_ref, own_ref, sums, held, arrived) = refs[:4], refs[4:]
    copies = [pltpu.make_async_copy(w, held.at[i], arrived.at[i]) for i, w in enumerate(weights)]
    for copy in copies:
        copy.start()
    n_y, rows, _ = out_ref.shape
    blocks, _, block, width = x_ref.shape
    core = place_ref[0]
    near = x_ref[:, core].reshape(blocks * block, width)
    far = x_ref[:, 1 - core].reshape(blocks * block, width)
    dims = (((1,), (1,)), ((), ()))
    for i in range(2):
        copies[2 * i].wait()
        part = lax.dot_general(near, held[2 * i], dims, preferred_element_type=F32)
        copies[2 * i + 1].wait()
        part = part + lax.dot_general(far, held[2 * i + 1], dims, preferred_element_type=F32)
        n = part.shape[1]
        part = part.reshape(n_y, rows, n)
        sums[:, :, i * n : (i + 1) * n] = part
        out_ref[:, :, i * n : (i + 1) * n] = part.astype(BF)
    own_ref[...] = sums[place_ref[1]]


def gate_up(place, x, g, g2, u, u2):
    blocks, _, block, width = x.shape
    hidden = g.shape[0]
    shape = (4, blocks * block // 4, 2 * hidden)
    return pl.pallas_call(
        gate_up_kernel,
        out_shape=[jax.ShapeDtypeStruct(shape, BF), jax.ShapeDtypeStruct(shape[1:], F32)],
        in_specs=[SMEM, VMEM] + [HBM] * 4,
        out_specs=[VMEM, VMEM],
        scratch_shapes=[
            pltpu.VMEM(shape, F32),
            pltpu.VMEM((4,) + g.shape, BF),
            pltpu.SemaphoreType.DMA((4,)),
        ],
        cost_estimate=pl.CostEstimate(flops=8 * blocks * block * width * hidden, bytes_accessed=10 << 20, transcendentals=0),
        compiler_params=params(50),
        name="gate_up",
    )(place, x, g, g2, u, u2)


def hidden_kernel(near_ref, far_ref, out_ref):
    total = near_ref[...] + far_ref[...].astype(F32)
    n = out_ref.shape[2]
    gate, up = total[:, :n], total[:, n:]
    value = (gate / (1.0 + jnp.exp(-gate)) * up).astype(BF)
    for i in range(out_ref.shape[0]):
        out_ref[i] = value


def hidden_copies(near, far, copies):
    rows, width = near.shape
    return pl.pallas_call(
        hidden_kernel,
        out_shape=jax.ShapeDtypeStruct((copies, rows, width // 2), BF),
        in_specs=[VMEM, VMEM],
        out_specs=VMEM,
        cost_estimate=pl.CostEstimate(flops=8 * rows * width, bytes_accessed=1 << 20, transcendentals=rows * width),
        compiler_params=params(8),
        name="hidden",
    )(near, far)


def down_kernel(place_ref, h_ref, w_ref, w2_ref, out_ref, own_ref, sums):
    blocks, _, block, width = out_ref.shape
    h = h_ref[...].reshape(blocks * block, h_ref.shape[2])
    for w, half in ((w_ref, place_ref[0]), (w2_ref, 1 - place_ref[0])):
        part = jnp.dot(h, w[...], preferred_element_type=F32).reshape(blocks, block, width)
        sums[:, half] = part
        out_ref[:, half] = part.astype(BF)
    own_ref[...] = sums[place_ref[2]]


def down(place, h, w, w2):
    hidden, width = w.shape
    rows = h.shape[0] * h.shape[1]
    shape = (8, 2, rows // 8, width)
    return pl.pallas_call(
        down_kernel,
        out_shape=[jax.ShapeDtypeStruct(shape, BF), jax.ShapeDtypeStruct(shape[1:], F32)],
        in_specs=[SMEM, VMEM, VMEM, VMEM],
        out_specs=[VMEM, VMEM],
        scratch_shapes=[pltpu.VMEM(shape, F32)],
        cost_estimate=pl.CostEstimate(flops=4 * rows * hidden * width, bytes_accessed=6 << 20, transcendentals=0),
        compiler_params=params(20),
        name="down",
    )(place, h, w, w2)


def block(tokens, gate_weight, up_weight, down_weight):
    rows, width = tokens.shape
    half = rows // 2
    at = {a: lax.axis_index(a).astype(jnp.int32) for a in ("y", "c", "x", "zp", "zq")}
    near, far = at["x"] * 2 + at["zp"], at["zq"] * 2 + at["c"]
    place = jnp.stack([at["c"], at["y"], near])
    far_y = [at["y"] != i for i in range(4)]
    far_near = [near != i for i in range(8)]
    mine = [at["c"] == i for i in range(2)]
    far_zq = [[(far != 2 * q + i) for q in range(4)] for i in range(2)]
    at, place, far_y, far_near, mine, far_zq, tokens = lax.optimization_barrier(
        (at, place, far_y, far_near, mine, far_zq, tokens)
    )

    gate_weight, up_weight = gate_weight.T, up_weight.T
    gate_other = lax.ppermute(gate_weight, "c", SWAP)
    up_other = lax.ppermute(up_weight, "c", SWAP)
    piece = jnp.broadcast_to(tokens.reshape(1, 2, half, width), (4, 2, half, width))
    piece = lax.all_to_all(piece.reshape(8, half, width), FAR, 0, 0).reshape(4, 2, half, width)
    piece = piece.transpose(1, 0, 2, 3).reshape(1, 2, 4 * half, width)
    piece = lax.all_to_all(jnp.broadcast_to(piece, (8, 2, 4 * half, width)), NEAR, 0, 0)

    parts, own = gate_up(place, piece, gate_weight, gate_other, up_weight, up_other)
    parts, own = lax.optimization_barrier((parts, own))
    summed = add_far(lax.all_to_all(parts, "y", 0, 0), far_y, own)
    rounded = summed.astype(BF)
    rounded, down_weight = lax.optimization_barrier((rounded, down_weight))
    other = lax.ppermute(rounded, "zh", SWAP)
    down_other = lax.ppermute(down_weight, "c", SWAP)
    hidden = lax.all_to_all(hidden_copies(summed, other, 4), "y", 0, 0)

    parts, own = down(place, hidden, down_weight, down_other)
    parts, own = lax.optimization_barrier((parts, own))
    out = add_far(lax.all_to_all(parts, NEAR, 0, 0), far_near, own)

    out = out.reshape(2, 4, half, width).transpose(1, 0, 2, 3)
    own = lax.dynamic_index_in_dim(out, at["zq"], 0, keepdims=False, allow_negative_indices=False)
    parts = out.astype(LAST).reshape(8, half, width)
    own = jnp.where(mine[0], own[0], own[1])
    parts, own = lax.optimization_barrier((parts, own))
    parts = lax.all_to_all(parts, FAR, 0, 0).reshape(4, 2, half, width)
    halves = [
        add_far(parts[:, i], far_zq[i], jnp.where(mine[i], own, 0.0)).astype(BF) for i in range(2)
    ]
    return jnp.concatenate(halves, axis=0)


def solution(mesh):
    sizes = [n for _, n in GX + GY]
    names = [a for a, _ in GX + GY]
    fine = Mesh(mesh.devices.reshape(sizes), names)
    gx, gy = tuple(a for a, _ in GX), tuple(a for a, _ in GY)
    return jax.shard_map(
        block,
        mesh=fine,
        in_specs=(P(gy, gx), P(gx, gy), P(gx, gy), P(gy, gx)),
        out_specs=P(gy, gx),
        check_vma=False,
    )
```

time: 866 us -> 150 us (0.17)
  the two profiles are of different devices: /device:TPU:16 before, /device:TPU:1 now
where the time goes in v3:
time: 150 us; the launch traced here: 149 us
  blocking collectives  83.2 us (55%)
  waiting for transfers between devices  28.9 us (19%)
  starting transfers between devices  25.4 us (17%)
  Pallas kernels  7.17 us (5%)
  local copies, waits for them, and re-layouts  3.12 us (2%)
    all_to_all x1, blocking collectives, block(): lax.all_to_all(piece.reshape(8, half, width), FAR, 0, 0)  22.2 us
    ppermute x1, waiting for transfers between devices, block(): other = lax.ppermute(rounded, 'zh', SWAP)  20.7 us
    all_to_all x1, blocking collectives, block(): out = add_far(lax.all_to_all(parts, NEAR, 0, 0), far_near, own)  19.9 us
    all_to_all x1, blocking collectives, block(): parts = lax.all_to_all(parts, FAR, 0, 0).reshape(4, 2, half, width)  16.8 us
    all_to_all x1, blocking collectives, block(): summed = add_far(lax.all_to_all(parts, 'y', 0, 0), far_y, own)  14.4 us
    all_to_all x1, blocking collectives, block(): hidden = lax.all_to_all(hidden_copies(summed, other, 4), 'y', 0, 0)  9.94 us
    ppermute x1, starting transfers between devices, block(): other = lax.ppermute(rounded, 'zh', SWAP)  8.06 us
    all_to_all x1, starting transfers between devices, block(): lax.all_to_all(jnp.broadcast_to(piece, (8, 2, 4 * half, width)), NEAR, 0, 0)  6.79 us
  transfers between devices with their start and end apart: 5, of which 4 were waited for; matrix products, arithmetic and copies ran while one was open for 0% of the time, Pallas kernels for 0%

profile of v3, /device:TPU:1, one launch (start us, length us, event | category | flops | bytes accessed | tf_op | source)
XLA Modules:
  0.0 149.0 jit_solution(4791671363910596662)
XLA Ops:
  0.0 0.1 pad_add_fusion.place_ref
  0.1 0.8 broadcast_in_dim.48
  0.8 22.2 %all_to_all.30 = bf16[8,8,1024]{2,1,0:T(8,128)(2,1)S(1)} all-to-all(bf16[8,8,1024]{2,1,0:T(8,128)(2,1)S(1)} %bitcast.111), channel_id=1, replica_groups=mesh['y'=4,'zh'=2,'c'=2,'x'=4,'zq'=4,'zp'=2] {'zq','c'}, dimensions={0} | all-to-all | bytes 262144 | tf_op jit(solution)/shard_map/all_to_all | solution.py:141
  23.1 0.0 copy-start.1
  23.1 1.1 broadcast_in_dim.50
  24.2 6.8 %all-to-all-start.1 = ((bf16[8,2,32,1024]{3,2,1,0:T(8,128)(2,1)}), bf16[8,2,32,1024]{3,2,1,0:T(8,128)(2,1)S(1)}, u32[]{:S(2)}, u32[]{:S(2)}) async-start(bf16[8,2,32,1024]{3,2,1,0:T(8,128)(2,1)} %broadcast_in_dim.50), calls=%async_computation.1 | async-start | bytes 2097152 | tf_op jit(solution)/shard_map/all_to_all | solution.py:143
  31.0 0.0 copy-done.1
  31.0 3.1 %collective-permute-start = (bf16[832,1024]{1,0:T(8,128)(2,1)S(1)}, bf16[832,1024]{1,0:T(8,128)(2,1)S(1)}, u32[]{:S(2)}, u32[]{:S(2)}) collective-permute-start(bf16[832,1024]{1,0:T(8,128)(2,1)S(1)} %bitcast.105), channel_id=1, source_target_pairs={{0,32},{32,0},{1,33},{33,1},{2,34},{34,2},{3,35},{35,3},{4,36},{36... | collective-permute-start | bytes 5111816 | tf_op jit(solution)/shard_map/ppermute | solution.py:138
  34.0 1.9 %collective-permute-start.1 = (bf16[832,1024]{1,0:T(8,128)(2,1)}, bf16[832,1024]{1,0:T(8,128)(2,1)}, u32[]{:S(2)}, u32[]{:S(2)}) collective-permute-start(bf16[832,1024]{1,0:T(8,128)(2,1)} %bitcast.107), channel_id=1, source_target_pairs={{0,32},{32,0},{1,33},{33,1},{2,34},{34,2},{3,35},{35,3},{4,36},{36... | collective-permute-start | bytes 5111816 | tf_op jit(solution)/shard_map/ppermute | solution.py:139
  36.0 1.3 collective-permute-done.refs_1_
  37.2 0.0 copy-start.2
  37.2 1.2 copy-done.2
  38.4 1.4 collective-permute-done.1.refs_3_
  39.9 5.5 %all-to-all-done.1.x_ref = bf16[8,2,32,1024]{3,2,1,0:T(8,128)(2,1)S(1)} async-done(((bf16[8,2,32,1024]{3,2,1,0:T(8,128)(2,1)}), bf16[8,2,32,1024]{3,2,1,0:T(8,128)(2,1)S(1)}, u32[]{:S(2)}, u32[]{:S(2)}) %all-to-all-start.1) | async-done | bytes 1048608 | tf_op jit(solution)/shard_map/all_to_all | solution.py:143
  45.3 5.2 %gate_up.1 = (bf16[4,64,1664]{2,1,0:T(8,128)(2,1)S(1)}, f32[64,1664]{1,0:T(8,128)S(1)}) custom-call(s32[3]{0:T(128)S(1)} %pad_add_fusion.place_ref, bf16[8,2,32,1024]{3,2,1,0:T(8,128)(2,1)S(1)} %all-to-all-done.1.x_ref, bf16[832,1024]{1,0:T(8,128)(2,1)S(1)} %bitcast.106, bf16[832,1024]{1,0:T(8,128)(2,1)} %copy-done.2, bf16[832,1024]{1,0:T(8,128)(2,1)} %bitcast.108, ...), custom_call_target="tpu_custom_call" | custom-call | flops 1744830464 | bytes 10485760 | tf_op jit(solution)/shard_map/gate_up/pallas_call | solution.py:59
  50.6 0.0 copy-start
  50.6 14.4 %all_to_all.31 = bf16[4,64,1664]{2,1,0:T(8,128)(2,1)S(1)} all-to-all(bf16[4,64,1664]{2,1,0:T(8,128)(2,1)S(1)} %get-tuple-element.43), channel_id=1, replica_groups=mesh['y'=4,'zh'=2,'c'=2,'x'=4,'zq'=4,'zp'=2] {'y'}, dimensions={0} | all-to-all | bytes 1703936 | tf_op jit(solution)/shard_map/all_to_all | solution.py:147
  64.9 0.2 fusion.4
  65.1 0.0 copy-done
  65.1 5.6 %collective-permute-start.3 = (bf16[832,1024]{1,0:T(8,128)(2,1)S(1)}, bf16[832,1024]{1,0:T(8,128)(2,1)S(1)}, u32[]{:S(2)}, u32[]{:S(2)}) collective-permute-start(bf16[832,1024]{1,0:T(8,128)(2,1)S(1)} %copy-done), channel_id=1, source_target_pairs={{0,32},{32,0},{1,33},{33,1},{2,34},{34,2},{3,35},{35,3},{4,36},{36... | collective-permute-start | bytes 5111816 | tf_op jit(solution)/shard_map/ppermute | solution.py:151
  70.7 8.1 %collective-permute-start.2 = (bf16[64,1664]{1,0:T(8,128)(2,1)S(1)}, bf16[64,1664]{1,0:T(8,128)(2,1)S(1)}, u32[]{:S(2)}, u32[]{:S(2)}) collective-permute-start(bf16[64,1664]{1,0:T(8,128)(2,1)S(1)} %get-tuple-element.47), channel_id=1, source_target_pairs={{0,64},{64,0},{1,65},{65,1},{2,66},{66,2},{3,67},{67,3},{4,68},{68... | collective-permute-start | bytes 638984 | tf_op jit(solution)/shard_map/ppermute | solution.py:150
  78.8 20.7 %collective-permute-done.2.far_ref = bf16[64,1664]{1,0:T(8,128)(2,1)S(1)} collective-permute-done((bf16[64,1664]{1,0:T(8,128)(2,1)S(1)}, bf16[64,1664]{1,0:T(8,128)(2,1)S(1)}, u32[]{:S(2)}, u32[]{:S(2)}) %collective-permute-start.2) | collective-permute-done | bytes 213024 | tf_op jit(solution)/shard_map/ppermute | solution.py:150
  99.5 0.1 hidden.1
  99.7 9.9 %all_to_all.32.h_ref = bf16[4,64,832]{2,1,0:T(8,128)(2,1)S(1)} all-to-all(bf16[4,64,832]{2,1,0:T(8,128)(2,1)S(1)} %hidden.1), channel_id=1, replica_groups=mesh['y'=4,'zh'=2,'c'=2,'x'=4,'zq'=4,'zp'=2] {'y'}, dimensions={0} | all-to-all | bytes 851968 | tf_op jit(solution)/shard_map/all_to_all | solution.py:152
  109.6 0.0 collective-permute-done.3.w2_ref
  109.6 1.8 %down.1 = (bf16[8,2,32,1024]{3,2,1,0:T(8,128)(2,1)S(1)}, f32[2,32,1024]{2,1,0:T(8,128)S(1)}) custom-call(s32[3]{0:T(128)S(1)} %pad_add_fusion.place_ref, bf16[4,64,832]{2,1,0:T(8,128)(2,1)S(1)} %all_to_all.32.h_ref, bf16[832,1024]{1,0:T(8,128)(2,1)S(1)} %copy-done, bf16[832,1024]{1,0:T(8,128)(2,1)S(1)} %collective-permute-done.3.w2_ref), custom_call_target="tpu_custom_call" | custom-call | flops 872415232 | bytes 6291456 | tf_op jit(solution)/shard_map/down/pallas_call | solution.py:111
  111.4 19.9 %all_to_all.33 = bf16[8,2,32,1024]{3,2,1,0:T(8,128)(2,1)S(1)} all-to-all(bf16[8,2,32,1024]{3,2,1,0:T(8,128)(2,1)S(1)} %get-tuple-element.51), channel_id=1, replica_groups=mesh['y'=4,'zh'=2,'c'=2,'x'=4,'zq'=4,'zp'=2] {'x','zp'}, dimensions={0} | all-to-all | bytes 2097152 | tf_op jit(solution)/shard_map/all_to_all | solution.py:156
  131.3 0.2 fusion
  131.6 16.8 %all_to_all.34 = bf16[8,8,1024]{2,1,0:T(8,128)(2,1)S(1)} all-to-all(bf16[8,8,1024]{2,1,0:T(8,128)(2,1)S(1)} %bitcast.109), channel_id=1, replica_groups=mesh['y'=4,'zh'=2,'c'=2,'x'=4,'zq'=4,'zp'=2] {'zq','c'}, dimensions={0} | all-to-all | bytes 262144 | tf_op jit(solution)/shard_map/all_to_all | solution.py:163
  148.4 0.6 pad_maximum_fusion
  (5 shorter events, 0.1 us)
Async XLA Ops:
  23.1 7.9 %copy-start.1 = (bf16[1024,832]{0,1:T(8,128)(2,1)S(1)}, bf16[1024,832]{0,1:T(8,128)(2,1)}, u32[]{:S(2)}) copy-start(bf16[1024,832]{0,1:T(8,128)(2,1)} %param.5) | copy-start | bytes 5111812
  24.2 21.1 %all-to-all-start.1 = ((bf16[8,2,32,1024]{3,2,1,0:T(8,128)(2,1)}), bf16[8,2,32,1024]{3,2,1,0:T(8,128)(2,1)S(1)}, u32[]{:S(2)}, u32[]{:S(2)}) async-start(bf16[8,2,32,1024]{3,2,1,0:T(8,128)(2,1)} %broadcast_in_dim.50), calls=%async_computation.1 | async-start | bytes 2097152 | tf_op jit(solution)/shard_map/all_to_all | solution.py:143
  31.0 6.3 %collective-permute-start = (bf16[832,1024]{1,0:T(8,128)(2,1)S(1)}, bf16[832,1024]{1,0:T(8,128)(2,1)S(1)}, u32[]{:S(2)}, u32[]{:S(2)}) collective-permute-start(bf16[832,1024]{1,0:T(8,128)(2,1)S(1)} %bitcast.105), channel_id=1, source_target_pairs={{0,32},{32,0},{1,33},{33,1},{2,34},{34,2},{3,35},{35,3},{4,36},{36... | collective-permute-start | bytes 5111816 | tf_op jit(solution)/shard_map/ppermute | solution.py:138
  34.0 5.8 %collective-permute-start.1 = (bf16[832,1024]{1,0:T(8,128)(2,1)}, bf16[832,1024]{1,0:T(8,128)(2,1)}, u32[]{:S(2)}, u32[]{:S(2)}) collective-permute-start(bf16[832,1024]{1,0:T(8,128)(2,1)} %bitcast.107), channel_id=1, source_target_pairs={{0,32},{32,0},{1,33},{33,1},{2,34},{34,2},{3,35},{35,3},{4,36},{36... | collective-permute-start | bytes 5111816 | tf_op jit(solution)/shard_map/ppermute | solution.py:139
  37.2 1.2 copy-start.2
  50.6 14.6 %copy-start = (bf16[832,1024]{1,0:T(8,128)(2,1)S(1)}, bf16[832,1024]{1,0:T(8,128)(2,1)}, u32[]{:S(2)}) copy-start(bf16[832,1024]{1,0:T(8,128)(2,1)} %w_ref) | copy-start | bytes 5111812
  65.1 44.5 %collective-permute-start.3 = (bf16[832,1024]{1,0:T(8,128)(2,1)S(1)}, bf16[832,1024]{1,0:T(8,128)(2,1)S(1)}, u32[]{:S(2)}, u32[]{:S(2)}) collective-permute-start(bf16[832,1024]{1,0:T(8,128)(2,1)S(1)} %copy-done), channel_id=1, source_target_pairs={{0,32},{32,0},{1,33},{33,1},{2,34},{34,2},{3,35},{35,3},{4,36},{36... | collective-permute-start | bytes 5111816 | tf_op jit(solution)/shard_map/ppermute | solution.py:151
  70.7 28.8 %collective-permute-start.2 = (bf16[64,1664]{1,0:T(8,128)(2,1)S(1)}, bf16[64,1664]{1,0:T(8,128)(2,1)S(1)}, u32[]{:S(2)}, u32[]{:S(2)}) collective-permute-start(bf16[64,1664]{1,0:T(8,128)(2,1)S(1)} %get-tuple-element.47), channel_id=1, source_target_pairs={{0,64},{64,0},{1,65},{65,1},{2,66},{66,2},{3,67},{67,3},{4,68},{68... | collective-permute-start | bytes 638984 | tf_op jit(solution)/shard_map/ppermute | solution.py:150

commit v4 on v3

--- a/solution.py
+++ b/solution.py
@@ -16,7 +16,6 @@
 SWAP = [(0, 1), (1, 0)]
 VMEM = pl.BlockSpec(memory_space=pltpu.VMEM)
 SMEM = pl.BlockSpec(memory_space=pltpu.SMEM)
-HBM = pl.BlockSpec(memory_space=pltpu.HBM)
 
 
 def params(mib):
@@ -29,22 +28,16 @@
     return own
 
 
-def gate_up_kernel(place_ref, x_ref, *refs):
-    weights, (out_ref, own_ref, sums, held, arrived) = refs[:4], refs[4:]
-    copies = [pltpu.make_async_copy(w, held.at[i], arrived.at[i]) for i, w in enumerate(weights)]
-    for copy in copies:
-        copy.start()
+def gate_up_kernel(place_ref, x_ref, g_ref, u_ref, g2_ref, u2_ref, out_ref, own_ref, sums):
     n_y, rows, _ = out_ref.shape
     blocks, _, block, width = x_ref.shape
     core = place_ref[0]
     near = x_ref[:, core].reshape(blocks * block, width)
     far = x_ref[:, 1 - core].reshape(blocks * block, width)
     dims = (((1,), (1,)), ((), ()))
-    for i in range(2):
-        copies[2 * i].wait()
-        part = lax.dot_general(near, held[2 * i], dims, preferred_element_type=F32)
-        copies[2 * i + 1].wait()
-        part = part + lax.dot_general(far, held[2 * i + 1], dims, preferred_element_type=F32)
+    for i, (w, w2) in enumerate(((g_ref, g2_ref), (u_ref, u2_ref))):
+        part = lax.dot_general(near, w[...], dims, preferred_element_type=F32)
+        part = part + lax.dot_general(far, w2[...], dims, preferred_element_type=F32)
         n = part.shape[1]
         part = part.reshape(n_y, rows, n)
         sums[:, :, i * n : (i + 1) * n] = part
@@ -52,24 +45,20 @@
     own_ref[...] = sums[place_ref[1]]
 
 
-def gate_up(place, x, g, g2, u, u2):
+def gate_up(place, x, g, u, g2, u2):
     blocks, _, block, width = x.shape
     hidden = g.shape[0]
     shape = (4, blocks * block // 4, 2 * hidden)
     return pl.pallas_call(
         gate_up_kernel,
         out_shape=[jax.ShapeDtypeStruct(shape, BF), jax.ShapeDtypeStruct(shape[1:], F32)],
-        in_specs=[SMEM, VMEM] + [HBM] * 4,
+        in_specs=[SMEM] + [VMEM] * 5,
         out_specs=[VMEM, VMEM],
-        scratch_shapes=[
-            pltpu.VMEM(shape, F32),
-            pltpu.VMEM((4,) + g.shape, BF),
-            pltpu.SemaphoreType.DMA((4,)),
-        ],
+        scratch_shapes=[pltpu.VMEM(shape, F32)],
         cost_estimate=pl.CostEstimate(flops=8 * blocks * block * width * hidden, bytes_accessed=10 << 20, transcendentals=0),
-        compiler_params=params(50),
+        compiler_params=params(20),
         name="gate_up",
-    )(place, x, g, g2, u, u2)
+    )(place, x, g, u, g2, u2)
 
 
 def hidden_kernel(near_ref, far_ref, out_ref):
@@ -138,11 +127,14 @@
     gate_other = lax.ppermute(gate_weight, "c", SWAP)
     up_other = lax.ppermute(up_weight, "c", SWAP)
     piece = jnp.broadcast_to(tokens.reshape(1, 2, half, width), (4, 2, half, width))
-    piece = lax.all_to_all(piece.reshape(8, half, width), FAR, 0, 0).reshape(4, 2, half, width)
+    piece = lax.all_to_all(piece.reshape(8, half, width), FAR, 0, 0)
+    piece = piece.reshape(4, 2, half, width)
+    piece, gate_other, up_other = lax.optimization_barrier((piece, gate_other, up_other))
     piece = piece.transpose(1, 0, 2, 3).reshape(1, 2, 4 * half, width)
-    piece = lax.all_to_all(jnp.broadcast_to(piece, (8, 2, 4 * half, width)), NEAR, 0, 0)
+    piece = jnp.broadcast_to(piece, (8, 2, 4 * half, width))
+    piece = lax.all_to_all(piece, NEAR, 0, 0)
 
-    parts, own = gate_up(place, piece, gate_weight, gate_other, up_weight, up_other)
+    parts, own = gate_up(place, piece, gate_weight, up_weight, gate_other, up_other)
     parts, own = lax.optimization_barrier((parts, own))
     summed = add_far(lax.all_to_all(parts, "y", 0, 0), far_y, own)
     rounded = summed.astype(BF)

time: 150 us -> 150 us (level)
  blocking collectives: 83.2 us -> 97.2 us
  waiting for transfers between devices: 28.9 us -> 20.9 us
  local copies, waits for them, and re-layouts: 3.12 us -> 0.94 us
  Pallas kernels: 7.17 us -> 5.04 us
  starting transfers between devices: 25.4 us -> 23.6 us
    all_to_all x1 -> x2, blocking collectives: 22.2 us -> 37.5 us  [the longest x1 21.6 us: block(): piece = lax.all_to_all(piece, NEAR, 0, 0)]
    all_to_all x1 -> x0, starting transfers between devices: 6.79 us -> none  [block(): lax.all_to_all(jnp.broadcast_to(piece, (8, 2, 4 * half, width)), NEAR, 0, 0)]
    ppermute x1, starting transfers between devices: 3.05 us -> 8.74 us  [block(): gate_other = lax.ppermute(gate_weight, 'c', SWAP)]
    all_to_all x1 -> x0, waiting for transfers between devices: 5.45 us -> none  [block(): lax.all_to_all(jnp.broadcast_to(piece, (8, 2, 4 * half, width)), NEAR, 0, 0)]
    pallas_call x1, Pallas kernels: 5.24 us -> 3.11 us  [gate_up(): pl.pallas_call(gate_up_kernel, out_shape=[jax.ShapeDtypeStruct(shape, BF)...]
    all_to_all x1, blocking collectives: 19.9 us -> 18.1 us  [block(): out = add_far(lax.all_to_all(parts, NEAR, 0, 0), far_near, own)]
  transfers between devices with their start and end apart: 5 -> 4, of which waited for: 4 -> 1; matrix products, arithmetic and copies ran while one was open for 0% -> 1% of each run, Pallas kernels for 0% -> 0%
where the time goes in v4:
time: 150 us; the launch traced here: 149 us
  blocking collectives  97.2 us (65%)
  starting transfers between devices  23.6 us (16%)
  waiting for transfers between devices  20.9 us (14%)
  Pallas kernels  5.04 us (3%)
    all_to_all x1, blocking collectives, block(): piece = lax.all_to_all(piece, NEAR, 0, 0)  21.6 us
    ppermute x1, waiting for transfers between devices, block(): other = lax.ppermute(rounded, 'zh', SWAP)  20.9 us
    all_to_all x1, blocking collectives, block(): out = add_far(lax.all_to_all(parts, NEAR, 0, 0), far_near, own)  18.1 us
    all_to_all x1, blocking collectives, block(): parts = lax.all_to_all(parts, FAR, 0, 0).reshape(4, 2, half, width)  16.8 us
    all_to_all x1, blocking collectives, block(): piece = lax.all_to_all(piece.reshape(8, half, width), FAR, 0, 0)  15.9 us
    all_to_all x1, blocking collectives, block(): summed = add_far(lax.all_to_all(parts, 'y', 0, 0), far_y, own)  14.9 us
    all_to_all x1, blocking collectives, block(): hidden = lax.all_to_all(hidden_copies(summed, other, 4), 'y', 0, 0)  9.95 us
    ppermute x1, starting transfers between devices, block(): gate_other = lax.ppermute(gate_weight, 'c', SWAP)  8.74 us
  transfers between devices with their start and end apart: 4, of which 1 were waited for; matrix products, arithmetic and copies ran while one was open for 1% of the time, Pallas kernels for 0%

profile of v4, /device:TPU:1, one launch (start us, length us, event | category | flops | bytes accessed | tf_op | source)
XLA Modules:
  0.0 149.0 jit_solution(18354245279265982881)
XLA Ops:
  0.0 8.7 %collective-permute-start = (bf16[832,1024]{1,0:T(8,128)(2,1)}, bf16[832,1024]{1,0:T(8,128)(2,1)S(1)}, u32[]{:S(2)}, u32[]{:S(2)}) collective-permute-start(bf16[832,1024]{1,0:T(8,128)(2,1)} %bitcast.105), channel_id=1, source_target_pairs={{0,32},{32,0},{1,33},{33,1},{2,34},{34,2},{3,35},{35,3},{4,36},{36... | collective-permute-start | bytes 5111816 | tf_op jit(solution)/shard_map/ppermute | solution.py:127
  8.7 1.9 %collective-permute-start.1 = (bf16[832,1024]{1,0:T(8,128)(2,1)}, bf16[832,1024]{1,0:T(8,128)(2,1)S(1)}, u32[]{:S(2)}, u32[]{:S(2)}) collective-permute-start(bf16[832,1024]{1,0:T(8,128)(2,1)} %bitcast.107), channel_id=1, source_target_pairs={{0,32},{32,0},{1,33},{33,1},{2,34},{34,2},{3,35},{35,3},{4,36},{36... | collective-permute-start | bytes 5111816 | tf_op jit(solution)/shard_map/ppermute | solution.py:128
  10.7 0.1 pad_add_fusion.place_ref
  10.8 0.8 broadcast_in_dim.48
  11.6 15.9 %all_to_all.30 = bf16[8,8,1024]{2,1,0:T(8,128)(2,1)S(1)} all-to-all(bf16[8,8,1024]{2,1,0:T(8,128)(2,1)S(1)} %bitcast.110), channel_id=1, replica_groups=mesh['y'=4,'zh'=2,'c'=2,'x'=4,'zq'=4,'zp'=2] {'zq','c'}, dimensions={0} | all-to-all | bytes 262144 | tf_op jit(solution)/shard_map/all_to_all | solution.py:130
  27.4 0.0 collective-permute-done.g2_ref
  27.4 0.0 collective-permute-done.1.u2_ref
  27.4 0.0 copy-start.2
  27.5 0.0 copy-start.1
  27.5 0.1 broadcast_in_dim.50
  27.6 21.6 %all_to_all.31.x_ref = bf16[8,2,32,1024]{3,2,1,0:T(8,128)(2,1)S(1)} all-to-all(bf16[8,2,32,1024]{3,2,1,0:T(8,128)(2,1)S(1)} %broadcast_in_dim.50), channel_id=1, replica_groups=mesh['y'=4,'zh'=2,'c'=2,'x'=4,'zq'=4,'zp'=2] {'x','zp'}, dimensions={0} | all-to-all | bytes 2097152 | tf_op jit(solution)/shard_map/all_to_all | solution.py:135
  49.2 0.0 copy-done.2
  49.2 0.0 copy-done.1
  49.2 3.1 %gate_up.1 = (bf16[4,64,1664]{2,1,0:T(8,128)(2,1)S(1)}, f32[64,1664]{1,0:T(8,128)S(1)}) custom-call(s32[3]{0:T(128)S(1)} %pad_add_fusion.place_ref, bf16[8,2,32,1024]{3,2,1,0:T(8,128)(2,1)S(1)} %all_to_all.31.x_ref, bf16[832,1024]{1,0:T(8,128)(2,1)S(1)} %bitcast.106, bf16[832,1024]{1,0:T(8,128)(2,1)S(1)} %bitcast.108, ...), custom_call_target="tpu_custom_call" | custom-call | flops 1744830464 | bytes 10485760 | tf_op jit(solution)/shard_map/gate_up/pallas_call | solution.py:52
  52.4 0.0 copy-start
  52.4 14.9 %all_to_all.32 = bf16[4,64,1664]{2,1,0:T(8,128)(2,1)S(1)} all-to-all(bf16[4,64,1664]{2,1,0:T(8,128)(2,1)S(1)} %get-tuple-element.49), channel_id=1, replica_groups=mesh['y'=4,'zh'=2,'c'=2,'x'=4,'zq'=4,'zp'=2] {'y'}, dimensions={0} | all-to-all | bytes 1703936 | tf_op jit(solution)/shard_map/all_to_all | solution.py:139
  67.3 0.2 fusion.4
  67.5 0.0 copy-done
  67.5 5.0 %collective-permute-start.3 = (bf16[832,1024]{1,0:T(8,128)(2,1)S(1)}, bf16[832,1024]{1,0:T(8,128)(2,1)S(1)}, u32[]{:S(2)}, u32[]{:S(2)}) collective-permute-start(bf16[832,1024]{1,0:T(8,128)(2,1)S(1)} %copy-done), channel_id=1, source_target_pairs={{0,32},{32,0},{1,33},{33,1},{2,34},{34,2},{3,35},{35,3},{4,36},{36... | collective-permute-start | bytes 5111816 | tf_op jit(solution)/shard_map/ppermute | solution.py:143
  72.5 7.9 %collective-permute-start.2 = (bf16[64,1664]{1,0:T(8,128)(2,1)S(1)}, bf16[64,1664]{1,0:T(8,128)(2,1)S(1)}, u32[]{:S(2)}, u32[]{:S(2)}) collective-permute-start(bf16[64,1664]{1,0:T(8,128)(2,1)S(1)} %get-tuple-element.53), channel_id=1, source_target_pairs={{0,64},{64,0},{1,65},{65,1},{2,66},{66,2},{3,67},{67,3},{4,68},{68... | collective-permute-start | bytes 638984 | tf_op jit(solution)/shard_map/ppermute | solution.py:142
  80.5 20.9 %collective-permute-done.2.far_ref = bf16[64,1664]{1,0:T(8,128)(2,1)S(1)} collective-permute-done((bf16[64,1664]{1,0:T(8,128)(2,1)S(1)}, bf16[64,1664]{1,0:T(8,128)(2,1)S(1)}, u32[]{:S(2)}, u32[]{:S(2)}) %collective-permute-start.2) | collective-permute-done | bytes 213024 | tf_op jit(solution)/shard_map/ppermute | solution.py:142
  101.4 0.1 hidden.1
  101.5 9.9 %all_to_all.33.h_ref = bf16[4,64,832]{2,1,0:T(8,128)(2,1)S(1)} all-to-all(bf16[4,64,832]{2,1,0:T(8,128)(2,1)S(1)} %hidden.1), channel_id=1, replica_groups=mesh['y'=4,'zh'=2,'c'=2,'x'=4,'zq'=4,'zp'=2] {'y'}, dimensions={0} | all-to-all | bytes 851968 | tf_op jit(solution)/shard_map/all_to_all | solution.py:144
  111.5 0.0 collective-permute-done.3.w2_ref
  111.5 1.8 %down.1 = (bf16[8,2,32,1024]{3,2,1,0:T(8,128)(2,1)S(1)}, f32[2,32,1024]{2,1,0:T(8,128)S(1)}) custom-call(s32[3]{0:T(128)S(1)} %pad_add_fusion.place_ref, bf16[4,64,832]{2,1,0:T(8,128)(2,1)S(1)} %all_to_all.33.h_ref, bf16[832,1024]{1,0:T(8,128)(2,1)S(1)} %copy-done, bf16[832,1024]{1,0:T(8,128)(2,1)S(1)} %collective-permute-done.3.w2_ref), custom_call_target="tpu_custom_call" | custom-call | flops 872415232 | bytes 6291456 | tf_op jit(solution)/shard_map/down/pallas_call | solution.py:100
  113.3 18.1 %all_to_all.34 = bf16[8,2,32,1024]{3,2,1,0:T(8,128)(2,1)S(1)} all-to-all(bf16[8,2,32,1024]{3,2,1,0:T(8,128)(2,1)S(1)} %get-tuple-element.57), channel_id=1, replica_groups=mesh['y'=4,'zh'=2,'c'=2,'x'=4,'zq'=4,'zp'=2] {'x','zp'}, dimensions={0} | all-to-all | bytes 2097152 | tf_op jit(solution)/shard_map/all_to_all | solution.py:148
  131.3 0.2 fusion
  131.6 16.8 %all_to_all.35 = bf16[8,8,1024]{2,1,0:T(8,128)(2,1)S(1)} all-to-all(bf16[8,8,1024]{2,1,0:T(8,128)(2,1)S(1)} %bitcast.109), channel_id=1, replica_groups=mesh['y'=4,'zh'=2,'c'=2,'x'=4,'zq'=4,'zp'=2] {'zq','c'}, dimensions={0} | all-to-all | bytes 262144 | tf_op jit(solution)/shard_map/all_to_all | solution.py:155
  148.4 0.6 pad_maximum_fusion
  (5 shorter events, 0.1 us)
Async XLA Ops:
  0.0 27.4 %collective-permute-start = (bf16[832,1024]{1,0:T(8,128)(2,1)}, bf16[832,1024]{1,0:T(8,128)(2,1)S(1)}, u32[]{:S(2)}, u32[]{:S(2)}) collective-permute-start(bf16[832,1024]{1,0:T(8,128)(2,1)} %bitcast.105), channel_id=1, source_target_pairs={{0,32},{32,0},{1,33},{33,1},{2,34},{34,2},{3,35},{35,3},{4,36},{36... | collective-permute-start | bytes 5111816 | tf_op jit(solution)/shard_map/ppermute | solution.py:127
  8.7 18.7 %collective-permute-start.1 = (bf16[832,1024]{1,0:T(8,128)(2,1)}, bf16[832,1024]{1,0:T(8,128)(2,1)S(1)}, u32[]{:S(2)}, u32[]{:S(2)}) collective-permute-start(bf16[832,1024]{1,0:T(8,128)(2,1)} %bitcast.107), channel_id=1, source_target_pairs={{0,32},{32,0},{1,33},{33,1},{2,34},{34,2},{3,35},{35,3},{4,36},{36... | collective-permute-start | bytes 5111816 | tf_op jit(solution)/shard_map/ppermute | solution.py:128
  27.4 21.8 %copy-start.2 = (bf16[1024,832]{0,1:T(8,128)(2,1)S(1)}, bf16[1024,832]{0,1:T(8,128)(2,1)}, u32[]{:S(2)}) copy-start(bf16[1024,832]{0,1:T(8,128)(2,1)} %param.6) | copy-start | bytes 5111812
  27.5 21.8 %copy-start.1 = (bf16[1024,832]{0,1:T(8,128)(2,1)S(1)}, bf16[1024,832]{0,1:T(8,128)(2,1)}, u32[]{:S(2)}) copy-start(bf16[1024,832]{0,1:T(8,128)(2,1)} %param.5) | copy-start | bytes 5111812
  52.4 15.1 %copy-start = (bf16[832,1024]{1,0:T(8,128)(2,1)S(1)}, bf16[832,1024]{1,0:T(8,128)(2,1)}, u32[]{:S(2)}) copy-start(bf16[832,1024]{1,0:T(8,128)(2,1)} %w_ref) | copy-start | bytes 5111812
  67.5 44.0 %collective-permute-start.3 = (bf16[832,1024]{1,0:T(8,128)(2,1)S(1)}, bf16[832,1024]{1,0:T(8,128)(2,1)S(1)}, u32[]{:S(2)}, u32[]{:S(2)}) collective-permute-start(bf16[832,1024]{1,0:T(8,128)(2,1)S(1)} %copy-done), channel_id=1, source_target_pairs={{0,32},{32,0},{1,33},{33,1},{2,34},{34,2},{3,35},{35,3},{4,36},{36... | collective-permute-start | bytes 5111816 | tf_op jit(solution)/shard_map/ppermute | solution.py:143
  72.5 28.8 %collective-permute-start.2 = (bf16[64,1664]{1,0:T(8,128)(2,1)S(1)}, bf16[64,1664]{1,0:T(8,128)(2,1)S(1)}, u32[]{:S(2)}, u32[]{:S(2)}) collective-permute-start(bf16[64,1664]{1,0:T(8,128)(2,1)S(1)} %get-tuple-element.53), channel_id=1, source_target_pairs={{0,64},{64,0},{1,65},{65,1},{2,66},{66,2},{3,67},{67,3},{4,68},{68... | collective-permute-start | bytes 638984 | tf_op jit(solution)/shard_map/ppermute | solution.py:142

commit v5 on v4

--- a/solution.py
+++ b/solution.py
@@ -14,8 +14,10 @@
 F32 = jnp.float32
 LAST = BF
 SWAP = [(0, 1), (1, 0)]
+PIECES = 4
 VMEM = pl.BlockSpec(memory_space=pltpu.VMEM)
 SMEM = pl.BlockSpec(memory_space=pltpu.SMEM)
+FREE = pl.BlockSpec(memory_space=pl.ANY)
 
 
 def params(mib):
@@ -28,18 +30,33 @@
     return own
 
 
-def gate_up_kernel(place_ref, x_ref, g_ref, u_ref, g2_ref, u2_ref, out_ref, own_ref, sums):
+def gate_up_kernel(place_ref, x_ref, *refs):
+    weights, (out_ref, own_ref, sums, held, arrived) = refs[:4], refs[4:]
+    n = weights[0].shape[0]
+    cuts = [(j * n // PIECES, (j + 1) * n // PIECES) for j in range(PIECES)]
+    copies = [
+        [
+            pltpu.make_async_copy(w.at[i:j], held.at[at, i:j], arrived.at[at, piece])
+            for piece, (i, j) in enumerate(cuts)
+        ]
+        for at, w in enumerate(weights)
+    ]
+    for at in (0, 2, 1, 3):
+        for copy in copies[at]:
+            copy.start()
     n_y, rows, _ = out_ref.shape
     blocks, _, block, width = x_ref.shape
     core = place_ref[0]
-    near = x_ref[:, core].reshape(blocks * block, width)
-    far = x_ref[:, 1 - core].reshape(blocks * block, width)
     dims = (((1,), (1,)), ((), ()))
-    for i, (w, w2) in enumerate(((g_ref, g2_ref), (u_ref, u2_ref))):
-        part = lax.dot_general(near, w[...], dims, preferred_element_type=F32)
-        part = part + lax.dot_general(far, w2[...], dims, preferred_element_type=F32)
-        n = part.shape[1]
-        part = part.reshape(n_y, rows, n)
+
+    def products(features, at):
+        for copy in copies[at]:
+            copy.wait()
+        x = x_ref[:, features].reshape(blocks * block, width)
+        return lax.dot_general(x, held[at], dims, preferred_element_type=F32).reshape(n_y, rows, n)
+
+    for i in range(2):
+        part = products(core, i) + products(1 - core, 2 + i)
         sums[:, :, i * n : (i + 1) * n] = part
         out_ref[:, :, i * n : (i + 1) * n] = part.astype(BF)
     own_ref[...] = sums[place_ref[1]]
@@ -52,11 +69,15 @@
     return pl.pallas_call(
         gate_up_kernel,
         out_shape=[jax.ShapeDtypeStruct(shape, BF), jax.ShapeDtypeStruct(shape[1:], F32)],
-        in_specs=[SMEM] + [VMEM] * 5,
+        in_specs=[SMEM, VMEM] + [FREE] * 4,
         out_specs=[VMEM, VMEM],
-        scratch_shapes=[pltpu.VMEM(shape, F32)],
+        scratch_shapes=[
+            pltpu.VMEM(shape, F32),
+            pltpu.VMEM((4,) + g.shape, BF),
+            pltpu.SemaphoreType.DMA((4, PIECES)),
+        ],
         cost_estimate=pl.CostEstimate(flops=8 * blocks * block * width * hidden, bytes_accessed=10 << 20, transcendentals=0),
-        compiler_params=params(20),
+        compiler_params=params(50),
         name="gate_up",
     )(place, x, g, u, g2, u2)
 
@@ -129,7 +150,6 @@
     piece = jnp.broadcast_to(tokens.reshape(1, 2, half, width), (4, 2, half, width))
     piece = lax.all_to_all(piece.reshape(8, half, width), FAR, 0, 0)
     piece = piece.reshape(4, 2, half, width)
-    piece, gate_other, up_other = lax.optimization_barrier((piece, gate_other, up_other))
     piece = piece.transpose(1, 0, 2, 3).reshape(1, 2, 4 * half, width)
     piece = jnp.broadcast_to(piece, (8, 2, 4 * half, width))
     piece = lax.all_to_all(piece, NEAR, 0, 0)

time: 150 us -> 150 us (level)
  blocking collectives: 97.2 us -> 83.2 us
  waiting for transfers between devices: 20.9 us -> 28.9 us
  Pallas kernels: 5.04 us -> 7.28 us
  local copies, waits for them, and re-layouts: 0.94 us -> 3.12 us
  starting transfers between devices: 23.6 us -> 25.4 us
    all_to_all x1 -> x0, blocking collectives: 21.6 us -> none  [block(): piece = lax.all_to_all(piece, NEAR, 0, 0)]
    all_to_all x0 -> x1, starting transfers between devices: none -> 6.79 us  [block(): piece = lax.all_to_all(piece, NEAR, 0, 0)]
    all_to_all x1, blocking collectives: 15.9 us -> 22.2 us  [block(): piece = lax.all_to_all(piece.reshape(8, half, width), FAR, 0, 0)]
    ppermute x1, starting transfers between devices: 8.74 us -> 3.05 us  [block(): gate_other = lax.ppermute(gate_weight, 'c', SWAP)]
    all_to_all x0 -> x1, waiting for transfers between devices: none -> 5.45 us  [block(): piece = lax.all_to_all(piece, NEAR, 0, 0)]
    pallas_call x1, Pallas kernels: 3.11 us -> 5.34 us  [gate_up(): pl.pallas_call(gate_up_kernel, out_shape=[jax.ShapeDtypeStruct(shape, BF)...]
    all_to_all x1, blocking collectives: 18.1 us -> 19.9 us  [block(): out = add_far(lax.all_to_all(parts, NEAR, 0, 0), far_near, own)]
  transfers between devices with their start and end apart: 4 -> 5, of which waited for: 1 -> 4; matrix products, arithmetic and copies ran while one was open for 1% -> 0% of each run, Pallas kernels for 0% -> 0%
where the time goes in v5:
time: 150 us; the launch traced here: 149 us
  blocking collectives  83.2 us (55%)
  waiting for transfers between devices  28.9 us (19%)
  starting transfers between devices  25.4 us (17%)
  Pallas kernels  7.28 us (5%)
  local copies, waits for them, and re-layouts  3.12 us (2%)
    all_to_all x1, blocking collectives, block(): piece = lax.all_to_all(piece.reshape(8, half, width), FAR, 0, 0)  22.2 us
    ppermute x1, waiting for transfers between devices, block(): other = lax.ppermute(rounded, 'zh', SWAP)  20.7 us
    all_to_all x1, blocking collectives, block(): out = add_far(lax.all_to_all(parts, NEAR, 0, 0), far_near, own)  19.9 us
    all_to_all x1, blocking collectives, block(): parts = lax.all_to_all(parts, FAR, 0, 0).reshape(4, 2, half, width)  16.8 us
    all_to_all x1, blocking collectives, block(): summed = add_far(lax.all_to_all(parts, 'y', 0, 0), far_y, own)  14.4 us
    all_to_all x1, blocking collectives, block(): hidden = lax.all_to_all(hidden_copies(summed, other, 4), 'y', 0, 0)  9.94 us
    ppermute x1, starting transfers between devices, block(): other = lax.ppermute(rounded, 'zh', SWAP)  8.07 us
    all_to_all x1, starting transfers between devices, block(): piece = lax.all_to_all(piece, NEAR, 0, 0)  6.79 us
  transfers between devices with their start and end apart: 5, of which 4 were waited for; matrix products, arithmetic and copies ran while one was open for 0% of the time, Pallas kernels for 0%

profile of v5, /device:TPU:1, one launch (start us, length us, event | category | flops | bytes accessed | tf_op | source)
XLA Modules:
  0.0 149.1 jit_solution(12572767944858068448)
XLA Ops:
  0.0 0.1 pad_add_fusion.place_ref
  0.1 0.8 broadcast_in_dim.48
  0.8 22.2 %all_to_all.30 = bf16[8,8,1024]{2,1,0:T(8,128)(2,1)S(1)} all-to-all(bf16[8,8,1024]{2,1,0:T(8,128)(2,1)S(1)} %bitcast.111), channel_id=1, replica_groups=mesh['y'=4,'zh'=2,'c'=2,'x'=4,'zq'=4,'zp'=2] {'zq','c'}, dimensions={0} | all-to-all | bytes 262144 | tf_op jit(solution)/shard_map/all_to_all | solution.py:151
  23.1 0.0 copy-start.1
  23.1 1.1 broadcast_in_dim.50
  24.2 6.8 %all-to-all-start.1 = ((bf16[8,2,32,1024]{3,2,1,0:T(8,128)(2,1)}), bf16[8,2,32,1024]{3,2,1,0:T(8,128)(2,1)S(1)}, u32[]{:S(2)}, u32[]{:S(2)}) async-start(bf16[8,2,32,1024]{3,2,1,0:T(8,128)(2,1)} %broadcast_in_dim.50), calls=%async_computation.1 | async-start | bytes 2097152 | tf_op jit(solution)/shard_map/all_to_all | solution.py:155
  31.0 0.0 copy-done.1
  31.0 3.1 %collective-permute-start = (bf16[832,1024]{1,0:T(8,128)(2,1)S(1)}, bf16[832,1024]{1,0:T(8,128)(2,1)S(1)}, u32[]{:S(2)}, u32[]{:S(2)}) collective-permute-start(bf16[832,1024]{1,0:T(8,128)(2,1)S(1)} %bitcast.105), channel_id=1, source_target_pairs={{0,32},{32,0},{1,33},{33,1},{2,34},{34,2},{3,35},{35,3},{4,36},{36... | collective-permute-start | bytes 5111816 | tf_op jit(solution)/shard_map/ppermute | solution.py:148
  34.0 1.9 %collective-permute-start.1 = (bf16[832,1024]{1,0:T(8,128)(2,1)}, bf16[832,1024]{1,0:T(8,128)(2,1)}, u32[]{:S(2)}, u32[]{:S(2)}) collective-permute-start(bf16[832,1024]{1,0:T(8,128)(2,1)} %bitcast.107), channel_id=1, source_target_pairs={{0,32},{32,0},{1,33},{33,1},{2,34},{34,2},{3,35},{35,3},{4,36},{36... | collective-permute-start | bytes 5111816 | tf_op jit(solution)/shard_map/ppermute | solution.py:149
  36.0 1.3 collective-permute-done.refs_2_
  37.2 0.0 copy-start.2
  37.2 1.2 copy-done.2
  38.4 1.4 collective-permute-done.1.refs_3_
  39.9 5.5 %all-to-all-done.1.x_ref = bf16[8,2,32,1024]{3,2,1,0:T(8,128)(2,1)S(1)} async-done(((bf16[8,2,32,1024]{3,2,1,0:T(8,128)(2,1)}), bf16[8,2,32,1024]{3,2,1,0:T(8,128)(2,1)S(1)}, u32[]{:S(2)}, u32[]{:S(2)}) %all-to-all-start.1) | async-done | bytes 1048608 | tf_op jit(solution)/shard_map/all_to_all | solution.py:155
  45.3 5.3 %gate_up.1 = (bf16[4,64,1664]{2,1,0:T(8,128)(2,1)S(1)}, f32[64,1664]{1,0:T(8,128)S(1)}) custom-call(s32[3]{0:T(128)S(1)} %pad_add_fusion.place_ref, bf16[8,2,32,1024]{3,2,1,0:T(8,128)(2,1)S(1)} %all-to-all-done.1.x_ref, bf16[832,1024]{1,0:T(8,128)(2,1)S(1)} %bitcast.106, bf16[832,1024]{1,0:T(8,128)(2,1)} %bitcast.108, bf16[832,1024]{1,0:T(8,128)(2,1)} %copy-done.2, ...), custom_call_target="tpu_custom_call" | custom-call | flops 1744830464 | bytes 10485760 | tf_op jit(solution)/shard_map/gate_up/pallas_call | solution.py:69
  50.7 0.0 copy-start
  50.7 14.4 %all_to_all.31 = bf16[4,64,1664]{2,1,0:T(8,128)(2,1)S(1)} all-to-all(bf16[4,64,1664]{2,1,0:T(8,128)(2,1)S(1)} %get-tuple-element.43), channel_id=1, replica_groups=mesh['y'=4,'zh'=2,'c'=2,'x'=4,'zq'=4,'zp'=2] {'y'}, dimensions={0} | all-to-all | bytes 1703936 | tf_op jit(solution)/shard_map/all_to_all | solution.py:159
  65.0 0.2 fusion.4
  65.2 0.0 copy-done
  65.2 5.6 %collective-permute-start.3 = (bf16[832,1024]{1,0:T(8,128)(2,1)S(1)}, bf16[832,1024]{1,0:T(8,128)(2,1)S(1)}, u32[]{:S(2)}, u32[]{:S(2)}) collective-permute-start(bf16[832,1024]{1,0:T(8,128)(2,1)S(1)} %copy-done), channel_id=1, source_target_pairs={{0,32},{32,0},{1,33},{33,1},{2,34},{34,2},{3,35},{35,3},{4,36},{36... | collective-permute-start | bytes 5111816 | tf_op jit(solution)/shard_map/ppermute | solution.py:163
  70.8 8.1 %collective-permute-start.2 = (bf16[64,1664]{1,0:T(8,128)(2,1)S(1)}, bf16[64,1664]{1,0:T(8,128)(2,1)S(1)}, u32[]{:S(2)}, u32[]{:S(2)}) collective-permute-start(bf16[64,1664]{1,0:T(8,128)(2,1)S(1)} %get-tuple-element.47), channel_id=1, source_target_pairs={{0,64},{64,0},{1,65},{65,1},{2,66},{66,2},{3,67},{67,3},{4,68},{68... | collective-permute-start | bytes 638984 | tf_op jit(solution)/shard_map/ppermute | solution.py:162
  78.9 20.7 %collective-permute-done.2.far_ref = bf16[64,1664]{1,0:T(8,128)(2,1)S(1)} collective-permute-done((bf16[64,1664]{1,0:T(8,128)(2,1)S(1)}, bf16[64,1664]{1,0:T(8,128)(2,1)S(1)}, u32[]{:S(2)}, u32[]{:S(2)}) %collective-permute-start.2) | collective-permute-done | bytes 213024 | tf_op jit(solution)/shard_map/ppermute | solution.py:162
  99.6 0.1 hidden.1
  99.8 9.9 %all_to_all.32.h_ref = bf16[4,64,832]{2,1,0:T(8,128)(2,1)S(1)} all-to-all(bf16[4,64,832]{2,1,0:T(8,128)(2,1)S(1)} %hidden.1), channel_id=1, replica_groups=mesh['y'=4,'zh'=2,'c'=2,'x'=4,'zq'=4,'zp'=2] {'y'}, dimensions={0} | all-to-all | bytes 851968 | tf_op jit(solution)/shard_map/all_to_all | solution.py:164
  109.7 0.0 collective-permute-done.3.w2_ref
  109.7 1.8 %down.1 = (bf16[8,2,32,1024]{3,2,1,0:T(8,128)(2,1)S(1)}, f32[2,32,1024]{2,1,0:T(8,128)S(1)}) custom-call(s32[3]{0:T(128)S(1)} %pad_add_fusion.place_ref, bf16[4,64,832]{2,1,0:T(8,128)(2,1)S(1)} %all_to_all.32.h_ref, bf16[832,1024]{1,0:T(8,128)(2,1)S(1)} %copy-done, bf16[832,1024]{1,0:T(8,128)(2,1)S(1)} %collective-permute-done.3.w2_ref), custom_call_target="tpu_custom_call" | custom-call | flops 872415232 | bytes 6291456 | tf_op jit(solution)/shard_map/down/pallas_call | solution.py:121
  111.5 19.9 %all_to_all.33 = bf16[8,2,32,1024]{3,2,1,0:T(8,128)(2,1)S(1)} all-to-all(bf16[8,2,32,1024]{3,2,1,0:T(8,128)(2,1)S(1)} %get-tuple-element.51), channel_id=1, replica_groups=mesh['y'=4,'zh'=2,'c'=2,'x'=4,'zq'=4,'zp'=2] {'x','zp'}, dimensions={0} | all-to-all | bytes 2097152 | tf_op jit(solution)/shard_map/all_to_all | solution.py:168
  131.4 0.2 fusion
  131.7 16.8 %all_to_all.34 = bf16[8,8,1024]{2,1,0:T(8,128)(2,1)S(1)} all-to-all(bf16[8,8,1024]{2,1,0:T(8,128)(2,1)S(1)} %bitcast.109), channel_id=1, replica_groups=mesh['y'=4,'zh'=2,'c'=2,'x'=4,'zq'=4,'zp'=2] {'zq','c'}, dimensions={0} | all-to-all | bytes 262144 | tf_op jit(solution)/shard_map/all_to_all | solution.py:175
  148.5 0.6 pad_maximum_fusion
  (5 shorter events, 0.1 us)
Async XLA Ops:
  23.1 7.9 %copy-start.1 = (bf16[1024,832]{0,1:T(8,128)(2,1)S(1)}, bf16[1024,832]{0,1:T(8,128)(2,1)}, u32[]{:S(2)}) copy-start(bf16[1024,832]{0,1:T(8,128)(2,1)} %param.5) | copy-start | bytes 5111812
  24.2 21.1 %all-to-all-start.1 = ((bf16[8,2,32,1024]{3,2,1,0:T(8,128)(2,1)}), bf16[8,2,32,1024]{3,2,1,0:T(8,128)(2,1)S(1)}, u32[]{:S(2)}, u32[]{:S(2)}) async-start(bf16[8,2,32,1024]{3,2,1,0:T(8,128)(2,1)} %broadcast_in_dim.50), calls=%async_computation.1 | async-start | bytes 2097152 | tf_op jit(solution)/shard_map/all_to_all | solution.py:155
  31.0 6.3 %collective-permute-start = (bf16[832,1024]{1,0:T(8,128)(2,1)S(1)}, bf16[832,1024]{1,0:T(8,128)(2,1)S(1)}, u32[]{:S(2)}, u32[]{:S(2)}) collective-permute-start(bf16[832,1024]{1,0:T(8,128)(2,1)S(1)} %bitcast.105), channel_id=1, source_target_pairs={{0,32},{32,0},{1,33},{33,1},{2,34},{34,2},{3,35},{35,3},{4,36},{36... | collective-permute-start | bytes 5111816 | tf_op jit(solution)/shard_map/ppermute | solution.py:148
  34.0 5.8 %collective-permute-start.1 = (bf16[832,1024]{1,0:T(8,128)(2,1)}, bf16[832,1024]{1,0:T(8,128)(2,1)}, u32[]{:S(2)}, u32[]{:S(2)}) collective-permute-start(bf16[832,1024]{1,0:T(8,128)(2,1)} %bitcast.107), channel_id=1, source_target_pairs={{0,32},{32,0},{1,33},{33,1},{2,34},{34,2},{3,35},{35,3},{4,36},{36... | collective-permute-start | bytes 5111816 | tf_op jit(solution)/shard_map/ppermute | solution.py:149
  37.2 1.2 copy-start.2
  50.7 14.6 %copy-start = (bf16[832,1024]{1,0:T(8,128)(2,1)S(1)}, bf16[832,1024]{1,0:T(8,128)(2,1)}, u32[]{:S(2)}) copy-start(bf16[832,1024]{1,0:T(8,128)(2,1)} %w_ref) | copy-start | bytes 5111812
  65.2 44.5 %collective-permute-start.3 = (bf16[832,1024]{1,0:T(8,128)(2,1)S(1)}, bf16[832,1024]{1,0:T(8,128)(2,1)S(1)}, u32[]{:S(2)}, u32[]{:S(2)}) collective-permute-start(bf16[832,1024]{1,0:T(8,128)(2,1)S(1)} %copy-done), channel_id=1, source_target_pairs={{0,32},{32,0},{1,33},{33,1},{2,34},{34,2},{3,35},{35,3},{4,36},{36... | collective-permute-start | bytes 5111816 | tf_op jit(solution)/shard_map/ppermute | solution.py:163
  70.8 28.8 %collective-permute-start.2 = (bf16[64,1664]{1,0:T(8,128)(2,1)S(1)}, bf16[64,1664]{1,0:T(8,128)(2,1)S(1)}, u32[]{:S(2)}, u32[]{:S(2)}) collective-permute-start(bf16[64,1664]{1,0:T(8,128)(2,1)S(1)} %get-tuple-element.47), channel_id=1, source_target_pairs={{0,64},{64,0},{1,65},{65,1},{2,66},{66,2},{3,67},{67,3},{4,68},{68... | collective-permute-start | bytes 638984 | tf_op jit(solution)/shard_map/ppermute | solution.py:162
